TPU v7x, 128 devices: a whole 4x4x4 slice. The times are simulated.
128 devices in a mesh: rows: 8 (over x, z_lo), cols: 16 (over y, z_hi, core).
Axes of the slice: x: 4, y: 4, z: 4 (z_hi: 2, z_lo: 2; z = z_hi * 2 + z_lo), core: 2. Of those that a mesh axis runs over, the one named last changes fastest.
Arguments:
- object_tiles: float32 [2, 2, 6144, 12288], P(None, None, 'rows', 'cols'), may hold values from -6 to 6
- probe: float32 [2, 512, 512], replicated, may hold values from -6 to 6
- prop_phase: float32 [512, 512], replicated, may hold values from -3.140625 to 3.140625
- amplitudes: bfloat16 [8, 16, 1, 512, 512], P('rows', 'cols'), may hold values from 0 to 2
- offsets: int32 [8, 16, 1, 2], P('rows', 'cols'), may hold values from 0 to 512
- counts: int32 [8, 16], P('rows', 'cols'), may hold values from 0 to 1
- step_size: float32 [2], replicated, may hold values from 0.3 to 1
Outputs:
- updated: float32 [2, 2, 6144, 12288], P(None, None, 'rows', 'cols')
Inputs may be any that keep to these rules, and one draw needn't show every extreme that they name: `offsets`: row and column of a window's first cell in the device's tile extended by 128 cells on every side. `counts`: slots at or past a tile's count are ignored; a tile may have no probe position.
All inputs are finite; a program needn't handle non-finite values.
Results may differ from a plain program's by a relative error of at most 0.013.
The roundings to bfloat16 on the way count: a program that leaves them out, or rounds other values in their place, can miss the bound.
Values sent between devices are 32-bit elements; how exact they have to be, the bound alone decides.
No kernel may reach another device: no remote copies, remote signals or barrier semaphores. Data moves between devices by JAX's collectives and lax.ppermute only.
A program may use at most 192 MiB of HBM per device.

v0:
```python
import math

import jax
import jax.numpy as jnp
from jax import lax
from jax.experimental import pallas as pl
from jax.experimental.pallas import tpu as pltpu
from jax.sharding import PartitionSpec as P

H = 128
W = 512
T = 768
B = 128
HALF = W // 2
LAST = T // H - 1
R0, C0, PR0, PC0, FR0, FC0, LIVE, ODD = range(8)

F32, BF16 = jnp.float32, jnp.bfloat16
WINDOW = jax.ShapeDtypeStruct((2, W, W), F32)
STRIP = jax.ShapeDtypeStruct((2, H, W), F32)
SIDE = jax.ShapeDtypeStruct((2, T, H), F32)


def rows_below(shape, first, limit):
    return lax.broadcasted_iota(jnp.int32, shape, 0) + first < limit


def cols_below(shape, first, limit):
    return lax.broadcasted_iota(jnp.int32, shape, 1) + first < limit


def params(limit_mib):
    return pltpu.CompilerParams(vmem_limit_bytes=limit_mib << 20)


def vmem():
    return pl.BlockSpec(memory_space=pltpu.VMEM)


def smem():
    return pl.BlockSpec(memory_space=pltpu.SMEM)


def prep_kernel(meta, probe, la, lai, rb, rbi, q):
    def table(rows, first_row, row_shift, col_shift):
        p = (lax.broadcasted_iota(jnp.int32, (rows, W), 0) + (first_row - row_shift)) & (W - 1)
        k = (lax.broadcasted_iota(jnp.int32, (rows, W), 1) - col_shift) & (W - 1)
        m = (p * k) & (W - 1)
        quadrant = (m + W // 8) >> 7
        x = (m - quadrant * (W // 4)).astype(F32) * (2.0 * math.pi / W)
        y = x * x
        s = x * (1.0 + y * (-1.0 / 6 + y * (1.0 / 120 + y * (-1.0 / 5040 + y * (1.0 / 362880)))))
        c = 1.0 + y * (-0.5 + y * (1.0 / 24 + y * (-1.0 / 720 + y * (1.0 / 40320 - y * (1.0 / 3628800)))))
        swap = (quadrant & 1) == 1
        cos = jnp.where(swap, s, c)
        sin = jnp.where(swap, c, s)
        cos = jnp.where(((quadrant + 1) & 2) == 2, -cos, cos)
        sin = jnp.where((quadrant & 2) == 2, -sin, sin)
        scaling = 1.0 / math.sqrt(W)
        return (cos * scaling).astype(BF16), (-sin * scaling).astype(BF16)

    r0, c0 = meta[R0], meta[C0]
    for first in range(0, W, B):
        rows = pl.ds(first, B)
        later = pl.ds(W + first, B)
        la[rows, :W], la[rows, W:] = table(B, first, 0, r0)
        lai[rows, :W], lai[rows, W:] = table(B, first, r0, 0)
        rb[rows, :], rb[later, :] = table(B, first, c0, 0)
        rbi[rows, :], rbi[later, :] = table(B, first, 0, c0)
    for part in range(2):
        q[part] = pltpu.roll(pltpu.roll(probe[part], r0 & (W - 1), 0), c0 & (W - 1), 1)


def prepare(meta, probe):
    return pl.pallas_call(
        prep_kernel,
        out_shape=[
            jax.ShapeDtypeStruct((W, 2 * W), BF16),
            jax.ShapeDtypeStruct((W, 2 * W), BF16),
            jax.ShapeDtypeStruct((2 * W, W), BF16),
            jax.ShapeDtypeStruct((2 * W, W), BF16),
            jax.ShapeDtypeStruct((2, W, W), F32),
        ],
        in_specs=[smem(), vmem()],
        out_specs=[vmem()] * 5,
        compiler_params=params(16),
        name="prepare",
    )(meta, probe)


def whole(kernel, name, out_shape, *operands, limit=16, **more):
    return pl.pallas_call(
        kernel,
        out_shape=out_shape,
        in_specs=[smem()] + [vmem()] * (len(operands) - 1),
        out_specs=[vmem()] * len(out_shape),
        compiler_params=params(limit),
        name=name,
        **more,
    )(*operands)


def edges(s, obj):
    return obj[s, :, :, :H], obj[s, :, :, T - H :]


def pack(tile, left, right, c0):
    shape = (tile.shape[0], H)
    middle = (tile.shape[0], W - 2 * H)
    a = jnp.where(cols_below(shape, 0, c0), tile[:, W - H : W], left)
    b = jnp.where(cols_below(middle, H, c0), tile[:, W:], tile[:, : W - 2 * H])
    c = jnp.where(cols_below(shape, W - H, c0), right, tile[:, W - 2 * H : W - H])
    return a, b, c


def put(out, rows, pieces):
    a, b, c = pieces
    out[rows, :H] = a
    out[rows, H : W - H] = b
    out[rows, W - H :] = c


def mate_takes(meta):
    upper = (meta[PR0] < HALF).astype(jnp.int32)
    return upper + meta[ODD] == 1


def far_takes(meta):
    upper = (meta[FR0] < HALF).astype(jnp.int32)
    return upper + meta[ODD] != 1


def pack_edge(out, s, obj, left, right, last, c0):
    rows = pl.ds(pl.multiple_of(last * (T - H), H), H)
    for part in range(2):
        put(out.at[part], slice(None), pack(obj[s, part, rows, :], left[part, rows, :], right[part, rows, :], c0))


def far_kernel(s, meta, obj, left, right, out):
    pack_edge(out, s, obj, left, right, meta[ODD], meta[FC0])


def mate_kernel(s, meta, obj, left, right, passing, out):
    own = mate_takes(meta)

    @pl.when(own)
    def _():
        pack_edge(out, s, obj, left, right, 1 - meta[ODD], meta[PC0])

    @pl.when(jnp.logical_not(own))
    def _():
        out[...] = passing[...]


def local_kernel(s, meta, obj, left, right, out):
    r0, c0 = meta[R0], meta[C0]
    for part in range(2):

        def packed(first):
            rows = pl.ds(first, B)
            return pack(obj[s, part, rows, :], left[part, rows, :], right[part, rows, :], c0)

        put(out.at[part], pl.ds(0, B), packed(W - H))
        for first in range(B, W - B, B):
            low, high = packed(first - H), packed(first + W - H)
            put(
                out.at[part],
                pl.ds(first, B),
                [jnp.where(rows_below(x.shape, first, r0), y, x) for x, y in zip(low, high)],
            )
        put(out.at[part], pl.ds(W - B, B), packed(W - B - H))


def window_rows(meta, local, strip, part, first):
    x = local[part, pl.ds(first, B), :]
    if first == 0:
        x = jnp.where(rows_below(x.shape, first, meta[R0]), x, strip[part])
    if first == W - B:
        x = jnp.where(rows_below(x.shape, first, meta[R0]), strip[part], x)
    return x


def put_left(v4, first, re, im, inverse):
    re, im = re.astype(BF16), im.astype(BF16)
    rows, later = pl.ds(first, B), pl.ds(W + first, B)
    v4[rows, :W] = re
    v4[rows, W:] = im
    v4[later, :W] = im if inverse else -im
    v4[later, W:] = -re if inverse else re


def left_product(table, v4, m4, inverse):
    for first in range(0, W, B):
        rows, later = pl.ds(first, B), pl.ds(W + first, B)
        mid = jnp.dot(table[rows, :], v4[...], preferred_element_type=F32).astype(BF16)
        re, im = mid[:, :W], mid[:, W:]
        m4[rows, :W] = re
        m4[rows, W:] = im if inverse else -im
        m4[later, :W] = im
        m4[later, W:] = -re if inverse else re


def right_product(m4, table, first):
    re = jnp.dot(m4[pl.ds(first, B), :], table[...], preferred_element_type=F32)
    im = jnp.dot(m4[pl.ds(W + first, B), :], table[...], preferred_element_type=F32)
    return re, im


def first_kernel(meta, local, strip, q, kern_re, kern_im, la, lai, rb, rbi, psi, v4, m4):
    for first in range(0, W, B):
        rows = pl.ds(first, B)
        o_re = window_rows(meta, local, strip, 0, first)
        o_im = window_rows(meta, local, strip, 1, first)
        q_re, q_im = q[0, rows, :], q[1, rows, :]
        put_left(v4, first, q_re * o_re - q_im * o_im, q_re * o_im + q_im * o_re, False)
    left_product(la, v4, m4, False)
    for first in range(0, W, B):
        rows = pl.ds(first, B)
        re, im = right_product(m4, rb, first)
        k_re, k_im = kern_re[rows, :], kern_im[rows, :]
        put_left(v4, first, re * k_re - im * k_im, re * k_im + im * k_re, True)
    left_product(lai, v4, m4, True)
    for first in range(0, W, B):
        rows = pl.ds(first, B)
        psi[0, rows, :], psi[1, rows, :] = right_product(m4, rbi, first)


def edge_rows(meta, g, zg):
    keep_first = meta[R0] < HALF
    live = meta[LIVE] > 0

    @pl.when(keep_first)
    def _():
        for part in range(2):
            x = g[part, :H, :]
            hide = rows_below(x.shape, 0, meta[R0])
            zg[part] = jnp.where(jnp.logical_and(live, jnp.logical_not(hide)), x, 0.0)

    @pl.when(jnp.logical_not(keep_first))
    def _():
        for part in range(2):
            x = g[part, W - H :, :]
            show = rows_below(x.shape, W - H, meta[R0])
            zg[part] = jnp.where(jnp.logical_and(live, show), x, 0.0)


def second_kernel(meta, local, strip, psi, amp, la, lai, rb, rbi, g2, back, zg, v4, m4):
    for first in range(0, W, B):
        rows = pl.ds(first, B)
        o_re = window_rows(meta, local, strip, 0, first)
        o_im = window_rows(meta, local, strip, 1, first)
        p_re, p_im = psi[0, rows, :], psi[1, rows, :]
        put_left(v4, first, p_re * o_re - p_im * o_im, p_re * o_im + p_im * o_re, False)
    left_product(la, v4, m4, False)
    for first in range(0, W, B):
        rows = pl.ds(first, B)
        re, im = right_product(m4, rb, first)
        factor = 1.0 - amp[rows, :].astype(F32) / jnp.sqrt(re * re + im * im + 1.0)
        put_left(v4, first, re * factor, im * factor, True)
    left_product(lai, v4, m4, True)
    for first in range(0, W, B):
        rows = pl.ds(first, B)
        re, im = right_product(m4, rbi, first)
        p_re, p_im = psi[0, rows, :], psi[1, rows, :]
        g2[0, rows, :] = p_re * re + p_im * im
        g2[1, rows, :] = p_re * im - p_im * re
        o_re = window_rows(meta, local, strip, 0, first)
        o_im = window_rows(meta, local, strip, 1, first)
        back[0, rows, :] = (o_re * re + o_im * im).astype(BF16)
        back[1, rows, :] = (o_re * im - o_im * re).astype(BF16)
    edge_rows(meta, g2, zg)


def third_kernel(meta, back, q, kern_re, kern_im, la, lai, rb, rbi, g1, zg, v4, m4):
    for first in range(0, W, B):
        rows = pl.ds(first, B)
        put_left(v4, first, back[0, rows, :], back[1, rows, :], False)
    left_product(la, v4, m4, False)
    for first in range(0, W, B):
        rows = pl.ds(first, B)
        re, im = right_product(m4, rb, first)
        k_re, k_im = kern_re[rows, :], kern_im[rows, :]
        put_left(v4, first, re * k_re + im * k_im, im * k_re - re * k_im, True)
    left_product(lai, v4, m4, True)
    for first in range(0, W, B):
        rows = pl.ds(first, B)
        re, im = right_product(m4, rbi, first)
        q_re, q_im = q[0, rows, :], q[1, rows, :]
        g1[0, rows, :] = q_re * re + q_im * im
        g1[1, rows, :] = q_re * im - q_im * re
    edge_rows(meta, g1, zg)


def transforms(kernel, name, out_shape, meta, *operands):
    return pl.pallas_call(
        kernel,
        out_shape=out_shape,
        in_specs=[smem()] + [vmem()] * len(operands),
        out_specs=[vmem()] * len(out_shape),
        scratch_shapes=[pltpu.VMEM((2 * W, 2 * W), BF16), pltpu.VMEM((2 * W, 2 * W), BF16)],
        compiler_params=params(16),
        name=name,
    )(meta, *operands)


def shares(meta, part, mate, far):
    odd = meta[ODD] > 0
    mate = jnp.where(mate_takes(meta), mate[part], 0.0)
    far = jnp.where(far_takes(meta), far[part], 0.0)
    top = jnp.where(odd, mate, far)
    bottom = jnp.where(odd, far, mate)
    c_top = jnp.where(odd, meta[PC0], meta[FC0])
    c_bottom = jnp.where(odd, meta[FC0], meta[PC0])
    return (top, c_top), (bottom, c_bottom)


def left_part(x, c0):
    x = x[:, :H]
    return jnp.where(cols_below(x.shape, 0, c0), 0.0, x)


def right_part(x, c0):
    x = x[:, W - H :]
    return jnp.where(cols_below(x.shape, W - H, c0), x, 0.0)


def inner_parts(x, c0):
    low, high = x[:, H:], x[:, : W - H]
    low = jnp.where(cols_below(low.shape, H, c0), 0.0, low)
    high = jnp.where(cols_below(high.shape, 0, c0), high, 0.0)
    return low, high


def tile_rows(meta, g, part, first):
    live = meta[LIVE] > 0
    if first < W - H:
        x = g[part, pl.ds(first + H, B), :]
        hide = rows_below(x.shape, first + H, meta[R0])
        return jnp.where(jnp.logical_and(live, jnp.logical_not(hide)), x, 0.0)
    x = g[part, pl.ds(first - (W - H), B), :]
    show = rows_below(x.shape, first - (W - H), meta[R0])
    return jnp.where(jnp.logical_and(live, show), x, 0.0)


def sides_kernel(meta, g, mate, far, to_left, to_right):
    for part in range(2):
        top, bottom = shares(meta, part, mate, far)
        for first in range(0, T, B):
            x = tile_rows(meta, g, part, first)
            a, b = left_part(x, meta[C0]), right_part(x, meta[C0])
            if first == 0:
                a, b = a + left_part(*top), b + right_part(*top)
            if first == T - B:
                a, b = a + left_part(*bottom), b + right_part(*bottom)
            to_left[part, pl.ds(first, B), :] = a
            to_right[part, pl.ds(first, B), :] = b


def update_kernel(s, meta, step, obj, g, mate, far, from_left, from_right, *rest):
    out, tile, sems = rest[-3:]
    size = step[s]
    copies = []
    for part in range(2):
        top, bottom = shares(meta, part, mate, far)
        for first in range(0, T, B):
            rows = pl.ds(first, B)
            low, high = inner_parts(tile_rows(meta, g, part, first), meta[C0])
            if first in (0, T - B):
                more = inner_parts(*(top if first == 0 else bottom))
                low, high = low + more[0], high + more[1]
            left = low[:, :H] + from_left[part, rows, :]
            right = high[:, W - 2 * H :] + from_right[part, rows, :]
            tile[part, rows, :H] = obj[s, part, rows, :H] - size * left
            tile[part, rows, H : W - H] = obj[s, part, rows, H : W - H] - size * low[:, H:]
            tile[part, rows, W - H : T - H] = obj[s, part, rows, W - H : T - H] - size * high[:, : W - 2 * H]
            tile[part, rows, T - H :] = obj[s, part, rows, T - H :] - size * right
            copy = pltpu.make_async_copy(tile.at[part, rows, :], out.at[s, part, rows, :], sems.at[part, first // B])
            copy.start()
            copies.append(copy)
    for copy in copies:
        copy.wait()


def update(s, meta, step, obj, g, mate, far, from_left, from_right, before):
    hbm = pl.BlockSpec(memory_space=pl.ANY)
    return pl.pallas_call(
        lambda *refs: update_kernel(s, *refs),
        out_shape=jax.ShapeDtypeStruct(obj.shape, F32),
        in_specs=[smem()] * 2 + [vmem()] * 6 + [hbm] * len(before),
        out_specs=hbm,
        scratch_shapes=[pltpu.VMEM((2, T, T), F32), pltpu.SemaphoreType.DMA((2, T // B))],
        input_output_aliases={8: 0} if before else {},
        compiler_params=params(16),
        name="update",
    )(meta, step, obj, g, mate, far, from_left, from_right, *before)


def per_device(object_tiles, probe, prop_phase, amplitudes, offsets, counts, step_size):
    n_rows, n_cols = lax.axis_size("rows"), lax.axis_size("cols")
    rightward = [(i, i + 1) for i in range(n_cols - 1)]
    leftward = [(i + 1, i) for i in range(n_cols - 1)]
    mates = [(i, i ^ 1) for i in range(n_rows) if i ^ 1 < n_rows]
    fars = [(i, i + 1) for i in range(1, n_rows - 1, 2)]
    fars = fars + [(j, i) for i, j in fars]
    inward = [(i, i - 2) for i in range(2, n_rows, 2)] + [(i, i + 2) for i in range(1, n_rows - 2, 2)]
    outward = [(j, i) for i, j in inward]

    own = offsets.reshape(2)
    odd = lax.axis_index("rows").astype(jnp.int32).reshape(1) & 1
    left, right = [None, None], [None, None]

    def send_edges(s, to_left, to_right):
        left[s] = lax.ppermute(to_right, "cols", rightward)
        right[s] = lax.ppermute(to_left, "cols", leftward)

    send_edges(0, *edges(0, object_tiles))
    beside = [lax.ppermute(own, "rows", mates), lax.ppermute(own, "rows", fars)]
    kernel = (jnp.cos(prop_phase), jnp.sin(prop_phase))
    ready = lax.optimization_barrier(
        (*edges(1, object_tiles), *beside, *prepare(own, probe), *kernel)
    )
    meta = jnp.concatenate([own, *ready[2:4], counts.reshape(1), odd])
    tables, q, kernel = ready[4:8], ready[8], ready[9:]
    send_edges(1, *ready[:2])

    local, strip = [], []
    for s in range(2):
        args = (meta, object_tiles, left[s], right[s])
        bind = lambda kernel, s=s: lambda *refs: kernel(s, *refs)
        (far,) = whole(bind(far_kernel), "far_strip", [STRIP], *args)
        passing = lax.ppermute(far, "rows", inward)
        (mate,) = whole(bind(mate_kernel), "mate_strip", [STRIP], *args, passing)
        strip.append(lax.ppermute(mate, "rows", mates))
        local += whole(bind(local_kernel), "local_window", [WINDOW], *args)

    (psi,) = transforms(first_kernel, "first", [WINDOW], meta, local[0], strip[0], q, *kernel, *tables)
    g2, back, z2 = transforms(
        second_kernel,
        "second",
        [WINDOW, jax.ShapeDtypeStruct((2, W, W), BF16), STRIP],
        meta,
        local[1],
        strip[1],
        psi,
        amplitudes[0, 0, 0],
        *tables,
    )
    g1, z1 = transforms(third_kernel, "third", [WINDOW, STRIP], meta, back, q, *kernel, *tables)

    out = ()
    for s, g, z in ((1, g2, z2), (0, g1, z1)):
        mate = lax.ppermute(z, "rows", mates)
        far = lax.ppermute(mate, "rows", outward)
        to_left, to_right = whole(sides_kernel, "sides", [SIDE] * 2, meta, g, mate, far)
        from_left = lax.ppermute(to_right, "cols", rightward)
        from_right = lax.ppermute(to_left, "cols", leftward)
        out = (update(s, meta, step_size, object_tiles, g, mate, far, from_left, from_right, out),)
    return out[0]


def solution(mesh):
    return jax.shard_map(
        per_device,
        mesh=mesh,
        in_specs=(
            P(None, None, "rows", "cols"),
            P(),
            P(),
            P("rows", "cols", None, None, None),
            P("rows", "cols", None, None),
            P("rows", "cols"),
            P(),
        ),
        out_specs=P(None, None, "rows", "cols"),
        check_vma=False,
    )
```

profile of v0, /device:TPU:19, one launch (start us, length us, event | category | flops | bytes accessed | tf_op | source)
XLA Modules:
  0.0 170.0 jit_solution(14096068299909509938)
XLA Ops:
  0.0 3.6 %collective-permute-start.1 = (s32[2]{0:T(128)}, s32[2]{0:T(128)S(1)}, u32[]{:S(2)}, u32[]{:S(2)}) collective-permute-start(s32[2]{0:T(128)} %bitcast.16), channel_id=1, source_target_pairs={{16,32},{48,64},{80,96},{32,16},{64,48},{96,80},{17,33},{49,65},{8... | collective-permute-start | bytes 32 | tf_op jit(solution)/shard_map/ppermute | solution.py:417
  4.5 3.6 %slice_bitcast_fusion = (f32[2,768,128]{2,1,0:T(8,128)}, f32[2,768,128]{2,1,0:T(8,128)}, f32[2,768,128]{2,1,0:T(8,128)}, f32[2,768,128]{2,1,0:T(8,128)}) fusion(f32[2,2,768,768]{3,2,1,0:T(8,128)} %refs_2_.3), kind=kLoop, calls=%fused_computation | loop fusion | bytes 6291456 | tf_op jit(solution)/shard_map/squeeze | solution.py:104
  8.1 3.3 %collective-permute-start.7 = (f32[2,768,128]{2,1,0:T(8,128)}, f32[2,768,128]{2,1,0:T(8,128)}, u32[]{:S(2)}, u32[]{:S(2)}) collective-permute-start(f32[2,768,128]{2,1,0:T(8,128)} %get-tuple-element.55), channel_id=1, source_target_pairs={{1,0},{2,1},{3,2},{4,3},{5,4},{6,5},{7,6},{8,7},{9,8},{10,9},{11,1... | collective-permute-start | bytes 2359304 | tf_op jit(solution)/shard_map/ppermute | solution.py:414
  11.4 5.4 %collective-permute-start.6 = (f32[2,768,128]{2,1,0:T(8,128)}, f32[2,768,128]{2,1,0:T(8,128)}, u32[]{:S(2)}, u32[]{:S(2)}) collective-permute-start(f32[2,768,128]{2,1,0:T(8,128)} %get-tuple-element.56), channel_id=1, source_target_pairs={{0,1},{1,2},{2,3},{3,4},{4,5},{5,6},{6,7},{7,8},{8,9},{9,10},{10,1... | collective-permute-start | bytes 2359304 | tf_op jit(solution)/shard_map/ppermute | solution.py:413
  16.8 3.7 %fusion = (f32[512,512]{1,0:T(8,128)S(1)}, f32[512,512]{1,0:T(8,128)S(1)}) fusion(f32[512,512]{1,0:T(8,128)S(1)} %copy-done.13), kind=kLoop, calls=%fused_computation.4 | loop fusion | bytes 3145728 | tf_op jit(solution)/shard_map/sin | solution.py:418
  20.5 11.3 %prepare.1 = (bf16[512,1024]{1,0:T(8,128)(2,1)S(1)}, bf16[512,1024]{1,0:T(8,128)(2,1)S(1)}, bf16[1024,512]{1,0:T(8,128)(2,1)S(1)}, bf16[1024,512]{1,0:T(8,128)(2,1)S(1)}, f32[2,512,512]{2,1,0:T(8,128)S(1)}) custom-call(s32[2]{0:T(128)S(1)} %bitcast.18, f32[2,512,512]{2,1,0:T(8,128)S(1)} %copy-done.9), custom_call_target="tpu_custom_call" | custom-call | tf_op jit(solution)/shard_map/prepare/pallas_call | solution.py:75
  36.1 2.4 %collective-permute-start.2 = (f32[2,768,128]{2,1,0:T(8,128)}, f32[2,768,128]{2,1,0:T(8,128)}, u32[]{:S(2)}, u32[]{:S(2)}) collective-permute-start(f32[2,768,128]{2,1,0:T(8,128)} %get-tuple-element.37), channel_id=1, source_target_pairs={{0,1},{1,2},{2,3},{3,4},{4,5},{5,6},{6,7},{7,8},{8,9},{9,10},{10,1... | collective-permute-start | bytes 2359304 | tf_op jit(solution)/shard_map/ppermute | solution.py:413
  38.5 1.9 %collective-permute-start.3 = (f32[2,768,128]{2,1,0:T(8,128)}, f32[2,768,128]{2,1,0:T(8,128)}, u32[]{:S(2)}, u32[]{:S(2)}) collective-permute-start(f32[2,768,128]{2,1,0:T(8,128)} %get-tuple-element.38), channel_id=1, source_target_pairs={{1,0},{2,1},{3,2},{4,3},{5,4},{6,5},{7,6},{8,7},{9,8},{10,9},{11,1... | collective-permute-start | bytes 2359304 | tf_op jit(solution)/shard_map/ppermute | solution.py:414
  41.2 3.7 %copy-done = f32[2,2,768,768]{3,2,1,0:T(8,128)S(1)} copy-done((f32[2,2,768,768]{3,2,1,0:T(8,128)S(1)}, f32[2,2,768,768]{3,2,1,0:T(8,128)}, u32[]{:S(2)}) %copy-start) | copy-done | bytes 9437208
  46.3 2.2 %collective-permute-start.8 = (f32[2,128,512]{2,1,0:T(8,128)S(1)}, f32[2,128,512]{2,1,0:T(8,128)S(1)}, u32[]{:S(2)}, u32[]{:S(2)}) collective-permute-start(f32[2,128,512]{2,1,0:T(8,128)S(1)} %far_strip.3), channel_id=1, source_target_pairs={{32,0},{64,32},{96,64},{16,48},{48,80},{80,112},{33,1},{65,33},{97... | collective-permute-start | bytes 1572872 | tf_op jit(solution)/shard_map/ppermute | solution.py:431
  48.5 7.7 %collective-permute-done.2.refs_2_ = f32[2,768,128]{2,1,0:T(8,128)} collective-permute-done((f32[2,768,128]{2,1,0:T(8,128)}, f32[2,768,128]{2,1,0:T(8,128)}, u32[]{:S(2)}, u32[]{:S(2)}) %collective-permute-start.2) | collective-permute-done | bytes 786464 | tf_op jit(solution)/shard_map/ppermute | solution.py:413
  56.1 2.9 %collective-permute-done.3.refs_3_ = f32[2,768,128]{2,1,0:T(8,128)} collective-permute-done((f32[2,768,128]{2,1,0:T(8,128)}, f32[2,768,128]{2,1,0:T(8,128)}, u32[]{:S(2)}, u32[]{:S(2)}) %collective-permute-start.3) | collective-permute-done | bytes 786464 | tf_op jit(solution)/shard_map/ppermute | solution.py:414
  60.5 2.2 %collective-permute-start.4 = (f32[2,128,512]{2,1,0:T(8,128)S(1)}, f32[2,128,512]{2,1,0:T(8,128)S(1)}, u32[]{:S(2)}, u32[]{:S(2)}) collective-permute-start(f32[2,128,512]{2,1,0:T(8,128)S(1)} %far_strip.2), channel_id=1, source_target_pairs={{32,0},{64,32},{96,64},{16,48},{48,80},{80,112},{33,1},{65,33},{97... | collective-permute-start | bytes 1572872 | tf_op jit(solution)/shard_map/ppermute | solution.py:431
  64.9 8.4 %collective-permute-done.4.refs_4_ = f32[2,128,512]{2,1,0:T(8,128)S(1)} collective-permute-done((f32[2,128,512]{2,1,0:T(8,128)S(1)}, f32[2,128,512]{2,1,0:T(8,128)S(1)}, u32[]{:S(2)}, u32[]{:S(2)}) %collective-permute-start.4) | collective-permute-done | bytes 524320 | tf_op jit(solution)/shard_map/ppermute | solution.py:431
  79.9 6.0 %first.1.psi = f32[2,512,512]{2,1,0:T(8,128)S(1)} custom-call(s32[8]{0:T(128)S(1)} %concatenate.3.refs_0_.meta, f32[2,512,512]{2,1,0:T(8,128)S(1)} %local_window.3.local, f32[2,128,512]{2,1,0:T(8,128)S(1)} %collective-permute-done.9.strip, f32[2,512,512]{2,1,0:T(8,128)S(1)} %copy-done.8, f32[512,512]{1,0:T(8,128)S(1)} %get-tuple-element.40.kern_re, ...), custom_call_target="tpu_custom_call" | custom-call | tf_op jit(solution)/shard_map/first/pallas_call | solution.py:295
  86.0 3.1 %collective-permute-done.5.strip = f32[2,128,512]{2,1,0:T(8,128)S(1)} collective-permute-done((f32[2,128,512]{2,1,0:T(8,128)S(1)}, f32[2,128,512]{2,1,0:T(8,128)S(1)}, u32[]{:S(2)}, u32[]{:S(2)}) %collective-permute-start.5) | collective-permute-done | bytes 524320 | tf_op jit(solution)/shard_map/ppermute | solution.py:433
  89.1 7.1 %second.1 = (f32[2,512,512]{2,1,0:T(8,128)S(1)}, bf16[2,512,512]{2,1,0:T(8,128)(2,1)S(1)}, f32[2,128,512]{2,1,0:T(8,128)S(1)}) custom-call(s32[8]{0:T(128)S(1)} %concatenate.3.refs_0_.meta, f32[2,512,512]{2,1,0:T(8,128)S(1)} %local_window.2.local, f32[2,128,512]{2,1,0:T(8,128)S(1)} %collective-permute-done.5.strip, f32[2,512,512]{2,1,0:T(8,128)S(1)} %first.1.psi, ...), custom_call_target="tpu_custom_call" | custom-call | tf_op jit(solution)/shard_map/second/pallas_call | solution.py:295
  96.6 5.7 %third.1 = (f32[2,512,512]{2,1,0:T(8,128)S(1)}, f32[2,128,512]{2,1,0:T(8,128)S(1)}) custom-call(s32[8]{0:T(128)S(1)} %concatenate.3.refs_0_.meta, bf16[2,512,512]{2,1,0:T(8,128)(2,1)S(1)} %get-tuple-element.46.back, f32[2,512,512]{2,1,0:T(8,128)S(1)} %copy-done.8, f32[512,512]{1,0:T(8,128)S(1)} %get-tuple-element.40.kern_re, ...), custom_call_target="tpu_custom_call" | custom-call | tf_op jit(solution)/shard_map/third/pallas_call | solution.py:295
  103.8 5.5 %collective-permute-done.14.mate.refs_4_ = f32[2,128,512]{2,1,0:T(8,128)S(1)} collective-permute-done((f32[2,128,512]{2,1,0:T(8,128)S(1)}, f32[2,128,512]{2,1,0:T(8,128)S(1)}, u32[]{:S(2)}, u32[]{:S(2)}) %collective-permute-start.14) | collective-permute-done | bytes 524320 | tf_op jit(solution)/shard_map/ppermute | solution.py:452
  109.3 3.4 %collective-permute-start.15 = (f32[2,128,512]{2,1,0:T(8,128)S(1)}, f32[2,128,512]{2,1,0:T(8,128)S(1)}, u32[]{:S(2)}, u32[]{:S(2)}) collective-permute-start(f32[2,128,512]{2,1,0:T(8,128)S(1)} %collective-permute-done.14.mate.refs_4_), channel_id=1, source_target_pairs={{0,32},{32,64},{64,96},{48,16},{80,48},{112,80},{1,33},{33,65},{65... | collective-permute-start | bytes 1572872 | tf_op jit(solution)/shard_map/ppermute | solution.py:453
  112.7 7.8 %collective-permute-done.10.mate.refs_4_ = f32[2,128,512]{2,1,0:T(8,128)S(1)} collective-permute-done((f32[2,128,512]{2,1,0:T(8,128)S(1)}, f32[2,128,512]{2,1,0:T(8,128)S(1)}, u32[]{:S(2)}, u32[]{:S(2)}) %collective-permute-start.10) | collective-permute-done | bytes 524320 | tf_op jit(solution)/shard_map/ppermute | solution.py:452
  120.5 3.4 %collective-permute-start.11 = (f32[2,128,512]{2,1,0:T(8,128)S(1)}, f32[2,128,512]{2,1,0:T(8,128)S(1)}, u32[]{:S(2)}, u32[]{:S(2)}) collective-permute-start(f32[2,128,512]{2,1,0:T(8,128)S(1)} %collective-permute-done.10.mate.refs_4_), channel_id=1, source_target_pairs={{0,32},{32,64},{64,96},{48,16},{80,48},{112,80},{1,33},{33,65},{65... | collective-permute-start | bytes 1572872 | tf_op jit(solution)/shard_map/ppermute | solution.py:453
  124.8 3.3 %collective-permute-start.16 = (f32[2,768,128]{2,1,0:T(8,128)S(1)}, f32[2,768,128]{2,1,0:T(8,128)S(1)}, u32[]{:S(2)}, u32[]{:S(2)}) collective-permute-start(f32[2,768,128]{2,1,0:T(8,128)S(1)} %get-tuple-element.53), channel_id=1, source_target_pairs={{0,1},{1,2},{2,3},{3,4},{4,5},{5,6},{6,7},{7,8},{8,9},{9,10},{10,1... | collective-permute-start | bytes 2359304 | tf_op jit(solution)/shard_map/ppermute | solution.py:455
  128.2 2.1 %collective-permute-start.17 = (f32[2,768,128]{2,1,0:T(8,128)S(1)}, f32[2,768,128]{2,1,0:T(8,128)S(1)}, u32[]{:S(2)}, u32[]{:S(2)}) collective-permute-start(f32[2,768,128]{2,1,0:T(8,128)S(1)} %get-tuple-element.54), channel_id=1, source_target_pairs={{1,0},{2,1},{3,2},{4,3},{5,4},{6,5},{7,6},{8,7},{9,8},{10,9},{11,1... | collective-permute-start | bytes 2359304 | tf_op jit(solution)/shard_map/ppermute | solution.py:456
  130.3 4.0 %collective-permute-done.11.far.refs_5_ = f32[2,128,512]{2,1,0:T(8,128)S(1)} collective-permute-done((f32[2,128,512]{2,1,0:T(8,128)S(1)}, f32[2,128,512]{2,1,0:T(8,128)S(1)}, u32[]{:S(2)}, u32[]{:S(2)}) %collective-permute-start.11) | collective-permute-done | bytes 524320 | tf_op jit(solution)/shard_map/ppermute | solution.py:453
  135.1 3.5 %collective-permute-start.12 = (f32[2,768,128]{2,1,0:T(8,128)S(1)}, f32[2,768,128]{2,1,0:T(8,128)S(1)}, u32[]{:S(2)}, u32[]{:S(2)}) collective-permute-start(f32[2,768,128]{2,1,0:T(8,128)S(1)} %get-tuple-element.49), channel_id=1, source_target_pairs={{0,1},{1,2},{2,3},{3,4},{4,5},{5,6},{6,7},{7,8},{8,9},{9,10},{10,1... | collective-permute-start | bytes 2359304 | tf_op jit(solution)/shard_map/ppermute | solution.py:455
  138.6 2.8 %collective-permute-start.13 = (f32[2,768,128]{2,1,0:T(8,128)S(1)}, f32[2,768,128]{2,1,0:T(8,128)S(1)}, u32[]{:S(2)}, u32[]{:S(2)}) collective-permute-start(f32[2,768,128]{2,1,0:T(8,128)S(1)} %get-tuple-element.50), channel_id=1, source_target_pairs={{1,0},{2,1},{3,2},{4,3},{5,4},{6,5},{7,6},{8,7},{9,8},{10,9},{11,1... | collective-permute-start | bytes 2359304 | tf_op jit(solution)/shard_map/ppermute | solution.py:456
  141.4 4.1 %collective-permute-done.16.refs_6_ = f32[2,768,128]{2,1,0:T(8,128)S(1)} collective-permute-done((f32[2,768,128]{2,1,0:T(8,128)S(1)}, f32[2,768,128]{2,1,0:T(8,128)S(1)}, u32[]{:S(2)}, u32[]{:S(2)}) %collective-permute-start.16) | collective-permute-done | bytes 786464 | tf_op jit(solution)/shard_map/ppermute | solution.py:455
  145.5 12.8 %collective-permute-done.17.refs_7_ = f32[2,768,128]{2,1,0:T(8,128)S(1)} collective-permute-done((f32[2,768,128]{2,1,0:T(8,128)S(1)}, f32[2,768,128]{2,1,0:T(8,128)S(1)}, u32[]{:S(2)}, u32[]{:S(2)}) %collective-permute-start.17) | collective-permute-done | bytes 786464 | tf_op jit(solution)/shard_map/ppermute | solution.py:456
  158.3 3.1 %update.2.refs_8_ = f32[2,2,768,768]{3,2,1,0:T(8,128)} custom-call(s32[8]{0:T(128)S(1)} %concatenate.3.refs_0_.meta, f32[2]{0:T(128)S(1)} %copy-done.11, f32[2,2,768,768]{3,2,1,0:T(8,128)S(1)} %bitcast.14, f32[2,512,512]{2,1,0:T(8,128)S(1)} %get-tuple-element.51.g.refs_3_, f32[2,128,512]{2,1,0:T(8,128)S(1)} %collective-permute-done.14.mate.refs_4_, ...), custom_call_target="tpu_custom_call" | custom-call | tf_op jit(solution)/shard_map/update/pallas_call | solution.py:386
  162.4 4.4 %collective-permute-done.13.refs_7_ = f32[2,768,128]{2,1,0:T(8,128)S(1)} collective-permute-done((f32[2,768,128]{2,1,0:T(8,128)S(1)}, f32[2,768,128]{2,1,0:T(8,128)S(1)}, u32[]{:S(2)}, u32[]{:S(2)}) %collective-permute-start.13) | collective-permute-done | bytes 786464 | tf_op jit(solution)/shard_map/ppermute | solution.py:456
  166.7 3.1 %update.3 = f32[2,2,768,768]{3,2,1,0:T(8,128)} custom-call(s32[8]{0:T(128)S(1)} %concatenate.3.refs_0_.meta, f32[2]{0:T(128)S(1)} %copy-done.11, f32[2,2,768,768]{3,2,1,0:T(8,128)S(1)} %bitcast.14, f32[2,512,512]{2,1,0:T(8,128)S(1)} %get-tuple-element.47.g.refs_3_, ...), custom_call_target="tpu_custom_call", output_to_operand_aliasing={{}: (8, {})} | custom-call | tf_op jit(solution)/shard_map/update/pallas_call | solution.py:386
  (56 shorter events, 21.3 us)
Async XLA Ops:
  0.0 16.8 %copy-start.13 = (f32[512,512]{1,0:T(8,128)S(1)}, f32[512,512]{1,0:T(8,128)}, u32[]{:S(2)}) copy-start(f32[512,512]{1,0:T(8,128)} %param.9) | copy-start | bytes 3145732
  0.0 36.1 %collective-permute-start.1 = (s32[2]{0:T(128)}, s32[2]{0:T(128)S(1)}, u32[]{:S(2)}, u32[]{:S(2)}) collective-permute-start(s32[2]{0:T(128)} %bitcast.16), channel_id=1, source_target_pairs={{16,32},{48,64},{80,96},{32,16},{64,48},{96,80},{17,33},{49,65},{8... | collective-permute-start | bytes 32 | tf_op jit(solution)/shard_map/ppermute | solution.py:417
  3.6 32.4 %collective-permute-start = (s32[2]{0:T(128)}, s32[2]{0:T(128)S(1)}, u32[]{:S(2)}, u32[]{:S(2)}) collective-permute-start(s32[2]{0:T(128)} %bitcast.17), channel_id=1, source_target_pairs={{0,16},{16,0},{32,48},{48,32},{64,80},{80,64},{96,112},{112,96},{1... | collective-permute-start | bytes 32 | tf_op jit(solution)/shard_map/ppermute | solution.py:417
  8.1 12.4 %copy-start.9 = (f32[2,512,512]{2,1,0:T(8,128)S(1)}, f32[2,512,512]{2,1,0:T(8,128)}, u32[]{:S(2)}) copy-start(f32[2,512,512]{2,1,0:T(8,128)} %probe.1) | copy-start | bytes 6291460
  8.1 12.4 %copy-start.12 = (s32[1,1,1,2]{3,2,1,0:T(1,128)S(1)}, s32[1,1,1,2]{3,2,1,0:T(1,128)}, u32[]{:S(2)}) copy-start(s32[1,1,1,2]{3,2,1,0:T(1,128)} %param.11) | copy-start | bytes 28
  8.1 33.0 %collective-permute-start.7 = (f32[2,768,128]{2,1,0:T(8,128)}, f32[2,768,128]{2,1,0:T(8,128)}, u32[]{:S(2)}, u32[]{:S(2)}) collective-permute-start(f32[2,768,128]{2,1,0:T(8,128)} %get-tuple-element.55), channel_id=1, source_target_pairs={{1,0},{2,1},{3,2},{4,3},{5,4},{6,5},{7,6},{8,7},{9,8},{10,9},{11,1... | collective-permute-start | bytes 2359304 | tf_op jit(solution)/shard_map/ppermute | solution.py:414
  11.4 29.8 %collective-permute-start.6 = (f32[2,768,128]{2,1,0:T(8,128)}, f32[2,768,128]{2,1,0:T(8,128)}, u32[]{:S(2)}, u32[]{:S(2)}) collective-permute-start(f32[2,768,128]{2,1,0:T(8,128)} %get-tuple-element.56), channel_id=1, source_target_pairs={{0,1},{1,2},{2,3},{3,4},{4,5},{5,6},{6,7},{7,8},{8,9},{9,10},{10,1... | collective-permute-start | bytes 2359304 | tf_op jit(solution)/shard_map/ppermute | solution.py:413
  34.8 1.3 copy-start.7
  36.1 20.1 %collective-permute-start.2 = (f32[2,768,128]{2,1,0:T(8,128)}, f32[2,768,128]{2,1,0:T(8,128)}, u32[]{:S(2)}, u32[]{:S(2)}) collective-permute-start(f32[2,768,128]{2,1,0:T(8,128)} %get-tuple-element.37), channel_id=1, source_target_pairs={{0,1},{1,2},{2,3},{3,4},{4,5},{5,6},{6,7},{7,8},{8,9},{9,10},{10,1... | collective-permute-start | bytes 2359304 | tf_op jit(solution)/shard_map/ppermute | solution.py:413
  38.5 20.5 %collective-permute-start.3 = (f32[2,768,128]{2,1,0:T(8,128)}, f32[2,768,128]{2,1,0:T(8,128)}, u32[]{:S(2)}, u32[]{:S(2)}) collective-permute-start(f32[2,768,128]{2,1,0:T(8,128)} %get-tuple-element.38), channel_id=1, source_target_pairs={{1,0},{2,1},{3,2},{4,3},{5,4},{6,5},{7,6},{8,7},{9,8},{10,9},{11,1... | collective-permute-start | bytes 2359304 | tf_op jit(solution)/shard_map/ppermute | solution.py:414
  41.2 3.7 %copy-start = (f32[2,2,768,768]{3,2,1,0:T(8,128)S(1)}, f32[2,2,768,768]{3,2,1,0:T(8,128)}, u32[]{:S(2)}) copy-start(f32[2,2,768,768]{3,2,1,0:T(8,128)} %refs_2_.3) | copy-start | bytes 28311556
  46.3 16.3 %collective-permute-start.8 = (f32[2,128,512]{2,1,0:T(8,128)S(1)}, f32[2,128,512]{2,1,0:T(8,128)S(1)}, u32[]{:S(2)}, u32[]{:S(2)}) collective-permute-start(f32[2,128,512]{2,1,0:T(8,128)S(1)} %far_strip.3), channel_id=1, source_target_pairs={{32,0},{64,32},{96,64},{16,48},{48,80},{80,112},{33,1},{65,33},{97... | collective-permute-start | bytes 1572872 | tf_op jit(solution)/shard_map/ppermute | solution.py:431
  60.5 12.9 %collective-permute-start.4 = (f32[2,128,512]{2,1,0:T(8,128)S(1)}, f32[2,128,512]{2,1,0:T(8,128)S(1)}, u32[]{:S(2)}, u32[]{:S(2)}) collective-permute-start(f32[2,128,512]{2,1,0:T(8,128)S(1)} %far_strip.2), channel_id=1, source_target_pairs={{32,0},{64,32},{96,64},{16,48},{48,80},{80,112},{33,1},{65,33},{97... | collective-permute-start | bytes 1572872 | tf_op jit(solution)/shard_map/ppermute | solution.py:431
  64.1 14.7 %collective-permute-start.9 = (f32[2,128,512]{2,1,0:T(8,128)S(1)}, f32[2,128,512]{2,1,0:T(8,128)S(1)}, u32[]{:S(2)}, u32[]{:S(2)}) collective-permute-start(f32[2,128,512]{2,1,0:T(8,128)S(1)} %mate_strip.3), channel_id=1, source_target_pairs={{0,16},{16,0},{32,48},{48,32},{64,80},{80,64},{96,112},{112,96},{1... | collective-permute-start | bytes 1572872 | tf_op jit(solution)/shard_map/ppermute | solution.py:433
  74.8 14.3 %collective-permute-start.5 = (f32[2,128,512]{2,1,0:T(8,128)S(1)}, f32[2,128,512]{2,1,0:T(8,128)S(1)}, u32[]{:S(2)}, u32[]{:S(2)}) collective-permute-start(f32[2,128,512]{2,1,0:T(8,128)S(1)} %mate_strip.2), channel_id=1, source_target_pairs={{0,16},{16,0},{32,48},{48,32},{64,80},{80,64},{96,112},{112,96},{1... | collective-permute-start | bytes 1572872 | tf_op jit(solution)/shard_map/ppermute | solution.py:433
  76.9 2.0 %copy-start.2 = (bf16[512,1024]{1,0:T(8,128)(2,1)S(1)}, bf16[512,1024]{1,0:T(8,128)(2,1)}, u32[]{:S(2)}) copy-start(bf16[512,1024]{1,0:T(8,128)(2,1)} %copy-done.1) | copy-start | bytes 3145732
  76.9 2.0 %copy-start.4 = (bf16[1024,512]{1,0:T(8,128)(2,1)S(1)}, bf16[1024,512]{1,0:T(8,128)(2,1)}, u32[]{:S(2)}) copy-start(bf16[1024,512]{1,0:T(8,128)(2,1)} %copy-done.3) | copy-start | bytes 3145732
  76.9 2.3 %copy-start.6 = (bf16[1024,512]{1,0:T(8,128)(2,1)S(1)}, bf16[1024,512]{1,0:T(8,128)(2,1)}, u32[]{:S(2)}) copy-start(bf16[1024,512]{1,0:T(8,128)(2,1)} %copy-done.5) | copy-start | bytes 3145732
  76.9 3.0 %copy-start.8 = (f32[2,512,512]{2,1,0:T(8,128)S(1)}, f32[2,512,512]{2,1,0:T(8,128)}, u32[]{:S(2)}) copy-start(f32[2,512,512]{2,1,0:T(8,128)} %copy-done.7) | copy-start | bytes 6291460
  78.8 10.3 %copy-start.10 = (bf16[1,1,1,512,512]{4,3,2,1,0:T(8,128)(2,1)S(1)}, bf16[1,1,1,512,512]{4,3,2,1,0:T(8,128)(2,1)}, u32[]{:S(2)}) copy-start(bf16[1,1,1,512,512]{4,3,2,1,0:T(8,128)(2,1)} %param.10) | copy-start | bytes 1572868
  89.1 69.2 %slice-start = ((s8[9437184]{0:T(1024)(128)(4,1)}), s8[4194304]{0:T(1024)(128)(4,1)S(1)}, s32[]{:S(2)}) async-start(s8[9437184]{0:T(1024)(128)(4,1)} %bitcast.13), calls=%async_computation | async-start | bytes 8388608
  89.1 69.2 %slice-start.1 = ((s8[9437184]{0:T(1024)(128)(4,1)}), s8[4194304]{0:T(1024)(128)(4,1)S(1)}, s32[]{:S(2)}) async-start(s8[9437184]{0:T(1024)(128)(4,1)} %bitcast.13), calls=%async_computation.1 | async-start | bytes 8388608
  96.2 13.1 %collective-permute-start.14 = (f32[2,128,512]{2,1,0:T(8,128)S(1)}, f32[2,128,512]{2,1,0:T(8,128)S(1)}, u32[]{:S(2)}, u32[]{:S(2)}) collective-permute-start(f32[2,128,512]{2,1,0:T(8,128)S(1)} %get-tuple-element.52), channel_id=1, source_target_pairs={{0,16},{16,0},{32,48},{48,32},{64,80},{80,64},{96,112},{112,96},{1... | collective-permute-start | bytes 1572872 | tf_op jit(solution)/shard_map/ppermute | solution.py:452
  96.6 61.8 %slice-start.2 = ((s8[9437184]{0:T(1024)(128)(4,1)}), s8[1048576]{0:T(1024)(128)(4,1)S(1)}, s32[]{:S(2)}) async-start(s8[9437184]{0:T(1024)(128)(4,1)} %bitcast.13), calls=%async_computation.2 | async-start | bytes 2097152
  102.3 18.2 %collective-permute-start.10 = (f32[2,128,512]{2,1,0:T(8,128)S(1)}, f32[2,128,512]{2,1,0:T(8,128)S(1)}, u32[]{:S(2)}, u32[]{:S(2)}) collective-permute-start(f32[2,128,512]{2,1,0:T(8,128)S(1)} %get-tuple-element.48), channel_id=1, source_target_pairs={{0,16},{16,0},{32,48},{48,32},{64,80},{80,64},{96,112},{112,96},{1... | collective-permute-start | bytes 1572872 | tf_op jit(solution)/shard_map/ppermute | solution.py:452
  109.3 14.7 %collective-permute-start.15 = (f32[2,128,512]{2,1,0:T(8,128)S(1)}, f32[2,128,512]{2,1,0:T(8,128)S(1)}, u32[]{:S(2)}, u32[]{:S(2)}) collective-permute-start(f32[2,128,512]{2,1,0:T(8,128)S(1)} %collective-permute-done.14.mate.refs_4_), channel_id=1, source_target_pairs={{0,32},{32,64},{64,96},{48,16},{80,48},{112,80},{1,33},{33,65},{65... | collective-permute-start | bytes 1572872 | tf_op jit(solution)/shard_map/ppermute | solution.py:453
  120.5 13.8 %collective-permute-start.11 = (f32[2,128,512]{2,1,0:T(8,128)S(1)}, f32[2,128,512]{2,1,0:T(8,128)S(1)}, u32[]{:S(2)}, u32[]{:S(2)}) collective-permute-start(f32[2,128,512]{2,1,0:T(8,128)S(1)} %collective-permute-done.10.mate.refs_4_), channel_id=1, source_target_pairs={{0,32},{32,64},{64,96},{48,16},{80,48},{112,80},{1,33},{33,65},{65... | collective-permute-start | bytes 1572872 | tf_op jit(solution)/shard_map/ppermute | solution.py:453
  124.8 33.5 %copy-start.11 = (f32[2]{0:T(128)S(1)}, f32[2]{0:T(128)}, u32[]{:S(2)}) copy-start(f32[2]{0:T(128)} %refs_1_.15) | copy-start | bytes 28
  124.8 20.7 %collective-permute-start.16 = (f32[2,768,128]{2,1,0:T(8,128)S(1)}, f32[2,768,128]{2,1,0:T(8,128)S(1)}, u32[]{:S(2)}, u32[]{:S(2)}) collective-permute-start(f32[2,768,128]{2,1,0:T(8,128)S(1)} %get-tuple-element.53), channel_id=1, source_target_pairs={{0,1},{1,2},{2,3},{3,4},{4,5},{5,6},{6,7},{7,8},{8,9},{9,10},{10,1... | collective-permute-start | bytes 2359304 | tf_op jit(solution)/shard_map/ppermute | solution.py:455
  128.2 30.2 %collective-permute-start.17 = (f32[2,768,128]{2,1,0:T(8,128)S(1)}, f32[2,768,128]{2,1,0:T(8,128)S(1)}, u32[]{:S(2)}, u32[]{:S(2)}) collective-permute-start(f32[2,768,128]{2,1,0:T(8,128)S(1)} %get-tuple-element.54), channel_id=1, source_target_pairs={{1,0},{2,1},{3,2},{4,3},{5,4},{6,5},{7,6},{8,7},{9,8},{10,9},{11,1... | collective-permute-start | bytes 2359304 | tf_op jit(solution)/shard_map/ppermute | solution.py:456
  135.1 27.2 %collective-permute-start.12 = (f32[2,768,128]{2,1,0:T(8,128)S(1)}, f32[2,768,128]{2,1,0:T(8,128)S(1)}, u32[]{:S(2)}, u32[]{:S(2)}) collective-permute-start(f32[2,768,128]{2,1,0:T(8,128)S(1)} %get-tuple-element.49), channel_id=1, source_target_pairs={{0,1},{1,2},{2,3},{3,4},{4,5},{5,6},{6,7},{7,8},{8,9},{9,10},{10,1... | collective-permute-start | bytes 2359304 | tf_op jit(solution)/shard_map/ppermute | solution.py:455
  138.6 28.1 %collective-permute-start.13 = (f32[2,768,128]{2,1,0:T(8,128)S(1)}, f32[2,768,128]{2,1,0:T(8,128)S(1)}, u32[]{:S(2)}, u32[]{:S(2)}) collective-permute-start(f32[2,768,128]{2,1,0:T(8,128)S(1)} %get-tuple-element.50), channel_id=1, source_target_pairs={{1,0},{2,1},{3,2},{4,3},{5,4},{6,5},{7,6},{8,7},{9,8},{10,9},{11,1... | collective-permute-start | bytes 2359304 | tf_op jit(solution)/shard_map/ppermute | solution.py:456
  (3 other events, 3.0 us)
where the time goes:
time: 171 us; the launch traced here: 170 us
  waiting for transfers between devices  61.6 us (36%)
  Pallas kernels  47.5 us (28%)
  starting transfers between devices  43.4 us (25%)
  local copies, waits for them, and re-layouts  16.4 us (10%)
    pallas_call x3, Pallas kernels, transforms(): pl.pallas_call(kernel, out_shape=out_shape, in_specs=[smem()] + [vmem()]...  18.8 us
    ppermute x2, waiting for transfers between devices, per_device(): from_right = lax.ppermute(to_left, 'cols', leftward)  17.2 us
    ppermute x2, waiting for transfers between devices, per_device(): mate = lax.ppermute(z, 'rows', mates)  13.3 us
    pallas_call x1, Pallas kernels, prepare(): pl.pallas_call(prep_kernel, out_shape=[jax.ShapeDtypeStruct((W, 2 * W), B...  11.3 us
    pallas_call x8, Pallas kernels, whole(): pl.pallas_call(kernel, out_shape=out_shape, in_specs=[smem()] + [vmem()]...  11.1 us
    unnamed x34, local copies, waits for them, and re-layouts  9.04 us
    ppermute x2, waiting for transfers between devices, per_device(): passing = lax.ppermute(far, 'rows', inward)  8.45 us
    ppermute x2, starting transfers between devices, send_edges(): left[s] = lax.ppermute(to_right, 'cols', rightward)  7.8 us
  transfers between devices with their start and end apart: 18, of which 11 were waited for; matrix products, arithmetic and copies ran while one was open for 4% of the time, Pallas kernels for 22%

commit v1 on v0

--- a/solution.py
+++ b/solution.py
@@ -41,51 +41,46 @@
     return pl.BlockSpec(memory_space=pltpu.SMEM)
 
 
-def prep_kernel(meta, probe, la, lai, rb, rbi, q):
-    def table(rows, first_row, row_shift, col_shift):
-        p = (lax.broadcasted_iota(jnp.int32, (rows, W), 0) + (first_row - row_shift)) & (W - 1)
-        k = (lax.broadcasted_iota(jnp.int32, (rows, W), 1) - col_shift) & (W - 1)
-        m = (p * k) & (W - 1)
-        quadrant = (m + W // 8) >> 7
-        x = (m - quadrant * (W // 4)).astype(F32) * (2.0 * math.pi / W)
-        y = x * x
-        s = x * (1.0 + y * (-1.0 / 6 + y * (1.0 / 120 + y * (-1.0 / 5040 + y * (1.0 / 362880)))))
-        c = 1.0 + y * (-0.5 + y * (1.0 / 24 + y * (-1.0 / 720 + y * (1.0 / 40320 - y * (1.0 / 3628800)))))
-        swap = (quadrant & 1) == 1
-        cos = jnp.where(swap, s, c)
-        sin = jnp.where(swap, c, s)
-        cos = jnp.where(((quadrant + 1) & 2) == 2, -cos, cos)
-        sin = jnp.where((quadrant & 2) == 2, -sin, sin)
-        scaling = 1.0 / math.sqrt(W)
-        return (cos * scaling).astype(BF16), (-sin * scaling).astype(BF16)
-
+def table(rows, first_row, row_shift, col_shift):
+    p = (lax.broadcasted_iota(jnp.int32, (rows, W), 0) + (first_row - row_shift)) & (W - 1)
+    k = (lax.broadcasted_iota(jnp.int32, (rows, W), 1) - col_shift) & (W - 1)
+    m = (p * k) & (W - 1)
+    quadrant = (m + W // 8) >> 7
+    x = (m - quadrant * (W // 4)).astype(F32) * (2.0 * math.pi / W)
+    y = x * x
+    s = x * (1.0 + y * (-1.0 / 6 + y * (1.0 / 120 + y * (-1.0 / 5040 + y * (1.0 / 362880)))))
+    c = 1.0 + y * (-0.5 + y * (1.0 / 24 + y * (-1.0 / 720 + y * (1.0 / 40320 - y * (1.0 / 3628800)))))
+    swap = (quadrant & 1) == 1
+    cos = jnp.where(swap, s, c)
+    sin = jnp.where(swap, c, s)
+    cos = jnp.where(((quadrant + 1) & 2) == 2, -cos, cos)
+    sin = jnp.where((quadrant & 2) == 2, -sin, sin)
+    scaling = 1.0 / math.sqrt(W)
+    return (cos * scaling).astype(BF16), (-sin * scaling).astype(BF16)
+
+
+def forward_kernel(meta, probe, la, rb, q):
     r0, c0 = meta[R0], meta[C0]
     for first in range(0, W, B):
         rows = pl.ds(first, B)
         later = pl.ds(W + first, B)
         la[rows, :W], la[rows, W:] = table(B, first, 0, r0)
-        lai[rows, :W], lai[rows, W:] = table(B, first, r0, 0)
         rb[rows, :], rb[later, :] = table(B, first, c0, 0)
-        rbi[rows, :], rbi[later, :] = table(B, first, 0, c0)
     for part in range(2):
         q[part] = pltpu.roll(pltpu.roll(probe[part], r0 & (W - 1), 0), c0 & (W - 1), 1)
 
 
-def prepare(meta, probe):
-    return pl.pallas_call(
-        prep_kernel,
-        out_shape=[
-            jax.ShapeDtypeStruct((W, 2 * W), BF16),
-            jax.ShapeDtypeStruct((W, 2 * W), BF16),
-            jax.ShapeDtypeStruct((2 * W, W), BF16),
-            jax.ShapeDtypeStruct((2 * W, W), BF16),
-            jax.ShapeDtypeStruct((2, W, W), F32),
-        ],
-        in_specs=[smem(), vmem()],
-        out_specs=[vmem()] * 5,
-        compiler_params=params(16),
-        name="prepare",
-    )(meta, probe)
+def inverse_kernel(meta, lai, rbi):
+    r0, c0 = meta[R0], meta[C0]
+    for first in range(0, W, B):
+        rows = pl.ds(first, B)
+        later = pl.ds(W + first, B)
+        lai[rows, :W], lai[rows, W:] = table(B, first, r0, 0)
+        rbi[rows, :], rbi[later, :] = table(B, first, 0, c0)
+
+
+LEFT = jax.ShapeDtypeStruct((W, 2 * W), BF16)
+RIGHT = jax.ShapeDtypeStruct((2 * W, W), BF16)
 
 
 def whole(kernel, name, out_shape, *operands, limit=16, **more):
@@ -130,45 +125,75 @@
     return upper + meta[ODD] != 1
 
 
-def pack_edge(out, s, obj, left, right, last, c0):
+def pack_edge(out, obj, left, right, last, c0):
     rows = pl.ds(pl.multiple_of(last * (T - H), H), H)
     for part in range(2):
-        put(out.at[part], slice(None), pack(obj[s, part, rows, :], left[part, rows, :], right[part, rows, :], c0))
-
-
-def far_kernel(s, meta, obj, left, right, out):
-    pack_edge(out, s, obj, left, right, meta[ODD], meta[FC0])
-
-
-def mate_kernel(s, meta, obj, left, right, passing, out):
+        put(out.at[part], slice(None), pack(obj[part], left[part, rows, :], right[part, rows, :], c0))
+
+
+def far_kernel(meta, obj, left, right, out):
+    pack_edge(out, obj, left, right, meta[ODD], meta[FC0])
+
+
+def mate_kernel(meta, obj, left, right, passing, out):
     own = mate_takes(meta)
 
     @pl.when(own)
     def _():
-        pack_edge(out, s, obj, left, right, 1 - meta[ODD], meta[PC0])
+        pack_edge(out, obj, left, right, 1 - meta[ODD], meta[PC0])
 
     @pl.when(jnp.logical_not(own))
     def _():
         out[...] = passing[...]
 
 
-def local_kernel(s, meta, obj, left, right, out):
+def local_kernel(meta, obj, left, right, out):
     r0, c0 = meta[R0], meta[C0]
-    for part in range(2):
-
-        def packed(first):
-            rows = pl.ds(first, B)
-            return pack(obj[s, part, rows, :], left[part, rows, :], right[part, rows, :], c0)
-
-        put(out.at[part], pl.ds(0, B), packed(W - H))
-        for first in range(B, W - B, B):
-            low, high = packed(first - H), packed(first + W - H)
-            put(
-                out.at[part],
-                pl.ds(first, B),
-                [jnp.where(rows_below(x.shape, first, r0), y, x) for x, y in zip(low, high)],
-            )
-        put(out.at[part], pl.ds(W - B, B), packed(W - B - H))
+    part = pl.program_id(0)
+
+    def packed(first):
+        rows = pl.ds(first, B)
+        return pack(obj[rows, :], left[part, rows, :], right[part, rows, :], c0)
+
+    put(out.at[part], pl.ds(0, B), packed(W - H))
+    for first in range(B, W - B, B):
+        low, high = packed(first - H), packed(first + W - H)
+        put(
+            out.at[part],
+            pl.ds(first, B),
+            [jnp.where(rows_below(x.shape, first, r0), y, x) for x, y in zip(low, high)],
+        )
+    put(out.at[part], pl.ds(W - B, B), packed(W - B - H))
+
+
+def on_tile(kernel, name, tile, steps, out_shape, meta, obj, *operands):
+    return pl.pallas_call(
+        kernel,
+        out_shape=out_shape,
+        grid_spec=pltpu.PrefetchScalarGridSpec(
+            num_scalar_prefetch=1,
+            grid=(steps,),
+            in_specs=[tile] + [vmem()] * len(operands),
+            out_specs=vmem(),
+        ),
+        compiler_params=params(52),
+        name=name,
+    )(meta, obj, *operands)
+
+
+def far_strip(s, *args):
+    tile = pl.BlockSpec((None, 2, H, T), lambda i, m: (s, 0, m[ODD] * LAST, 0))
+    return on_tile(far_kernel, "far_strip", tile, 1, STRIP, *args)
+
+
+def mate_strip(s, *args):
+    tile = pl.BlockSpec((None, 2, H, T), lambda i, m: (s, 0, (1 - m[ODD]) * LAST, 0))
+    return on_tile(mate_kernel, "mate_strip", tile, 1, STRIP, *args)
+
+
+def local_window(s, *args):
+    tile = pl.BlockSpec((None, None, T, T), lambda i, m: (s, i, 0, 0))
+    return on_tile(local_kernel, "local_window", tile, 2, WINDOW, *args)
 
 
 def window_rows(meta, local, strip, part, first):
@@ -413,25 +438,27 @@
         left[s] = lax.ppermute(to_right, "cols", rightward)
         right[s] = lax.ppermute(to_left, "cols", leftward)
 
-    send_edges(0, *edges(0, object_tiles))
     beside = [lax.ppermute(own, "rows", mates), lax.ppermute(own, "rows", fars)]
+    first, *starts = lax.optimization_barrier((own, *edges(0, object_tiles)))
+    send_edges(0, *starts)
+    forward = whole(forward_kernel, "forward_tables", [LEFT, RIGHT, WINDOW], first, probe)
     kernel = (jnp.cos(prop_phase), jnp.sin(prop_phase))
-    ready = lax.optimization_barrier(
-        (*edges(1, object_tiles), *beside, *prepare(own, probe), *kernel)
-    )
-    meta = jnp.concatenate([own, *ready[2:4], counts.reshape(1), odd])
-    tables, q, kernel = ready[4:8], ready[8], ready[9:]
-    send_edges(1, *ready[:2])
+    ready = lax.optimization_barrier((object_tiles, *forward, *kernel, *beside))
+    obj, la, rb, q = ready[:4]
+    kernel, beside = ready[4:6], ready[6:]
+    second, *starts = lax.optimization_barrier((own, *edges(1, obj)))
+    send_edges(1, *starts)
+    lai, rbi = whole(inverse_kernel, "inverse_tables", [LEFT, RIGHT], second)
+    meta = jnp.concatenate([own, *beside, counts.reshape(1), odd])
+    tables = (la, lai, rb, rbi)
+    left[0], right[0], *tables = lax.optimization_barrier((left[0], right[0], *tables))
 
     local, strip = [], []
     for s in range(2):
         args = (meta, object_tiles, left[s], right[s])
-        bind = lambda kernel, s=s: lambda *refs: kernel(s, *refs)
-        (far,) = whole(bind(far_kernel), "far_strip", [STRIP], *args)
-        passing = lax.ppermute(far, "rows", inward)
-        (mate,) = whole(bind(mate_kernel), "mate_strip", [STRIP], *args, passing)
-        strip.append(lax.ppermute(mate, "rows", mates))
-        local += whole(bind(local_kernel), "local_window", [WINDOW], *args)
+        passing = lax.ppermute(far_strip(s, *args), "rows", inward)
+        strip.append(lax.ppermute(mate_strip(s, *args, passing), "rows", mates))
+        local.append(local_window(s, *args))
 
     (psi,) = transforms(first_kernel, "first", [WINDOW], meta, local[0], strip[0], q, *kernel, *tables)
     g2, back, z2 = transforms(

time: 171 us -> 179 us (1.047)
  Pallas kernels: 47.5 us -> 59.4 us
  waiting for transfers between devices: 61.6 us -> 55.2 us
  starting transfers between devices: 43.4 us -> 46.6 us
    pallas_call x1 -> x6, Pallas kernels: 11.3 us -> 20.5 us  [on_tile(): pl.pallas_call(kernel, out_shape=out_shape, grid_spec=pltpu.PrefetchScala...]
    ppermute x2, starting transfers between devices: 7.8 us -> 11.9 us  [send_edges(): left[s] = lax.ppermute(to_right, 'cols', rightward)]
    ppermute x2, waiting for transfers between devices: 7.68 us -> 4.56 us  [send_edges(): left[s] = lax.ppermute(to_right, 'cols', rightward)]
    unnamed x34 -> x36, local copies, waits for them, and re-layouts: 9.04 us -> 6.04 us
    ppermute x2, waiting for transfers between devices: 17.2 us -> 15 us  [per_device(): from_right = lax.ppermute(to_left, 'cols', leftward)]
    ppermute x2, waiting for transfers between devices: 4.96 us -> 7.07 us  [per_device(): from_left = lax.ppermute(to_right, 'cols', rightward)]
    squeeze x1 -> x2, local copies, waits for them, and re-layouts: 3.61 us -> 5.26 us  [edges(): return (obj[s, :, :, :H], obj[s, :, :, T - H:])]
    pallas_call x8 -> x4, Pallas kernels: 11.1 us -> 12.2 us  [whole(): pl.pallas_call(kernel, out_shape=out_shape, in_specs=[smem()] + [vmem()]...]
  transfers between devices with their start and end apart: 18 -> 18, of which waited for: 11 -> 11; matrix products, arithmetic and copies ran while one was open for 4% -> 5% of each run, Pallas kernels for 22% -> 27%
where the time goes in v1:
time: 179 us; the launch traced here: 178 us
  Pallas kernels  59.4 us (33%)
  waiting for transfers between devices  55.2 us (31%)
  starting transfers between devices  46.6 us (26%)
  local copies, waits for them, and re-layouts  15.1 us (8%)
    pallas_call x6, Pallas kernels, on_tile(): pl.pallas_call(kernel, out_shape=out_shape, grid_spec=pltpu.PrefetchScala...  20.5 us
    pallas_call x3, Pallas kernels, transforms(): pl.pallas_call(kernel, out_shape=out_shape, in_specs=[smem()] + [vmem()]...  20.5 us
    ppermute x2, waiting for transfers between devices, per_device(): from_right = lax.ppermute(to_left, 'cols', leftward)  15 us
    ppermute x2, waiting for transfers between devices, per_device(): mate = lax.ppermute(z, 'rows', mates)  13.4 us
    pallas_call x4, Pallas kernels, whole(): pl.pallas_call(kernel, out_shape=out_shape, in_specs=[smem()] + [vmem()]...  12.2 us
    ppermute x2, starting transfers between devices, send_edges(): left[s] = lax.ppermute(to_right, 'cols', rightward)  11.9 us
    ppermute x2, waiting for transfers between devices, per_device(): passing = lax.ppermute(far_strip(s, *args), 'rows', inward)  10.2 us
    ppermute x2, starting transfers between devices, per_device(): from_left = lax.ppermute(to_right, 'cols', rightward)  8.28 us
  transfers between devices with their start and end apart: 18, of which 11 were waited for; matrix products, arithmetic and copies ran while one was open for 5% of the time, Pallas kernels for 27%

profile of v1, /device:TPU:19, one launch (start us, length us, event | category | flops | bytes accessed | tf_op | source)
XLA Modules:
  0.0 177.5 jit_solution(7936741525775758181)
XLA Ops:
  0.0 3.6 %collective-permute-start.1 = (s32[2]{0:T(128)}, s32[2]{0:T(128)S(1)}, u32[]{:S(2)}, u32[]{:S(2)}) collective-permute-start(s32[2]{0:T(128)} %bitcast.16), channel_id=1, source_target_pairs={{16,32},{48,64},{80,96},{32,16},{64,48},{96,80},{17,33},{49,65},{8... | collective-permute-start | bytes 32 | tf_op jit(solution)/shard_map/ppermute | solution.py:441
  4.5 2.6 %slice_bitcast_fusion.2 = (f32[2,768,128]{2,1,0:T(8,128)}, f32[2,768,128]{2,1,0:T(8,128)}) fusion(f32[2,2,768,768]{3,2,1,0:T(8,128)} %refs_2_.3), kind=kLoop, calls=%fused_computation.2 | loop fusion | bytes 3145728 | tf_op jit(solution)/shard_map/squeeze | solution.py:99
  7.2 6.7 %collective-permute-start.6 = (f32[2,768,128]{2,1,0:T(8,128)}, f32[2,768,128]{2,1,0:T(8,128)}, u32[]{:S(2)}, u32[]{:S(2)}) collective-permute-start(f32[2,768,128]{2,1,0:T(8,128)} %get-tuple-element.48), channel_id=1, source_target_pairs={{0,1},{1,2},{2,3},{3,4},{4,5},{5,6},{6,7},{7,8},{8,9},{9,10},{10,1... | collective-permute-start | bytes 2359304 | tf_op jit(solution)/shard_map/ppermute | solution.py:438
  15.9 3.7 %fusion = (f32[512,512]{1,0:T(8,128)S(1)}, f32[512,512]{1,0:T(8,128)S(1)}) fusion(f32[512,512]{1,0:T(8,128)S(1)} %copy-done.14), kind=kLoop, calls=%fused_computation.4 | loop fusion | bytes 3145728 | tf_op jit(solution)/shard_map/sin | solution.py:445
  19.6 6.6 %forward_tables.1 = (bf16[512,1024]{1,0:T(8,128)(2,1)S(1)}, bf16[1024,512]{1,0:T(8,128)(2,1)S(1)}, f32[2,512,512]{2,1,0:T(8,128)S(1)}) custom-call(s32[2]{0:T(128)S(1)} %bitcast.18, f32[2,512,512]{2,1,0:T(8,128)S(1)} %copy-done.10), custom_call_target="tpu_custom_call" | custom-call | tf_op jit(solution)/shard_map/forward_tables/pallas_call | solution.py:87
  28.5 2.6 %slice_bitcast_fusion = (f32[2,768,128]{2,1,0:T(8,128)}, f32[2,768,128]{2,1,0:T(8,128)}) fusion(f32[2,2,768,768]{3,2,1,0:T(8,128)} %refs_2_.3), kind=kLoop, calls=%fused_computation | loop fusion | bytes 3145728 | tf_op jit(solution)/shard_map/squeeze | solution.py:99
  31.1 5.1 %collective-permute-start.2 = (f32[2,768,128]{2,1,0:T(8,128)}, f32[2,768,128]{2,1,0:T(8,128)}, u32[]{:S(2)}, u32[]{:S(2)}) collective-permute-start(f32[2,768,128]{2,1,0:T(8,128)} %get-tuple-element.46), channel_id=1, source_target_pairs={{0,1},{1,2},{2,3},{3,4},{4,5},{5,6},{6,7},{7,8},{8,9},{9,10},{10,1... | collective-permute-start | bytes 2359304 | tf_op jit(solution)/shard_map/ppermute | solution.py:438
  39.0 3.9 %inverse_tables.1 = (bf16[512,1024]{1,0:T(8,128)(2,1)S(1)}, bf16[1024,512]{1,0:T(8,128)(2,1)S(1)}) custom-call(s32[2]{0:T(128)S(1)} %bitcast.19), custom_call_target="tpu_custom_call" | custom-call | tf_op jit(solution)/shard_map/inverse_tables/pallas_call | solution.py:87
  45.0 2.2 %far_strip.3 = f32[2,128,512]{2,1,0:T(8,128)S(1)} custom-call(s32[8]{0:T(128)S(1)} %concatenate.3.meta.refs_0_, f32[2,2,768,768]{3,2,1,0:T(8,128)} %refs_2_.3, f32[2,768,128]{2,1,0:T(8,128)} %collective-permute-done.6.left, f32[2,768,128]{2,1,0:T(8,128)} %collective-permute-done.7.right), custom_call_target="tpu_custom_call" | custom-call | tf_op jit(solution)/shard_map/far_strip/pallas_call | solution.py:170
  49.3 4.6 %collective-permute-done.2.left = f32[2,768,128]{2,1,0:T(8,128)} collective-permute-done((f32[2,768,128]{2,1,0:T(8,128)}, f32[2,768,128]{2,1,0:T(8,128)}, u32[]{:S(2)}, u32[]{:S(2)}) %collective-permute-start.2) | collective-permute-done | bytes 786464 | tf_op jit(solution)/shard_map/ppermute | solution.py:438
  55.5 2.2 %far_strip.2 = f32[2,128,512]{2,1,0:T(8,128)S(1)} custom-call(s32[8]{0:T(128)S(1)} %concatenate.3.meta.refs_0_, f32[2,2,768,768]{3,2,1,0:T(8,128)} %refs_2_.3, f32[2,768,128]{2,1,0:T(8,128)} %collective-permute-done.2.left, f32[2,768,128]{2,1,0:T(8,128)} %collective-permute-done.3.right), custom_call_target="tpu_custom_call" | custom-call | tf_op jit(solution)/shard_map/far_strip/pallas_call | solution.py:170
  60.9 3.0 %mate_strip.3 = f32[2,128,512]{2,1,0:T(8,128)} custom-call(s32[8]{0:T(128)S(1)} %concatenate.3.meta.refs_0_, f32[2,2,768,768]{3,2,1,0:T(8,128)} %refs_2_.3, f32[2,768,128]{2,1,0:T(8,128)} %collective-permute-done.6.left, f32[2,768,128]{2,1,0:T(8,128)} %collective-permute-done.7.right, f32[2,128,512]{2,1,0:T(8,128)S(1)} %collective-permute-done.8.passing), custom_call_target="tpu_custom_call" | custom-call | tf_op jit(solution)/shard_map/mate_strip/pallas_call | solution.py:170
  64.6 9.2 %collective-permute-done.4.passing = f32[2,128,512]{2,1,0:T(8,128)S(1)} collective-permute-done((f32[2,128,512]{2,1,0:T(8,128)S(1)}, f32[2,128,512]{2,1,0:T(8,128)S(1)}, u32[]{:S(2)}, u32[]{:S(2)}) %collective-permute-start.4) | collective-permute-done | bytes 524320 | tf_op jit(solution)/shard_map/ppermute | solution.py:459
  73.7 3.0 %mate_strip.2 = f32[2,128,512]{2,1,0:T(8,128)} custom-call(s32[8]{0:T(128)S(1)} %concatenate.3.meta.refs_0_, f32[2,2,768,768]{3,2,1,0:T(8,128)} %refs_2_.3, f32[2,768,128]{2,1,0:T(8,128)} %collective-permute-done.2.left, f32[2,768,128]{2,1,0:T(8,128)} %collective-permute-done.3.right, f32[2,128,512]{2,1,0:T(8,128)S(1)} %collective-permute-done.4.passing), custom_call_target="tpu_custom_call" | custom-call | tf_op jit(solution)/shard_map/mate_strip/pallas_call | solution.py:170
  77.1 4.9 %local_window.3.local = f32[2,512,512]{2,1,0:T(8,128)} custom-call(s32[8]{0:T(128)S(1)} %concatenate.3.meta.refs_0_, f32[2,2,768,768]{3,2,1,0:T(8,128)} %refs_2_.3, f32[2,768,128]{2,1,0:T(8,128)} %collective-permute-done.6.left, f32[2,768,128]{2,1,0:T(8,128)} %collective-permute-done.7.right), custom_call_target="tpu_custom_call" | custom-call | tf_op jit(solution)/shard_map/local_window/pallas_call | solution.py:170
  82.1 5.2 %local_window.2.local = f32[2,512,512]{2,1,0:T(8,128)} custom-call(s32[8]{0:T(128)S(1)} %concatenate.3.meta.refs_0_, f32[2,2,768,768]{3,2,1,0:T(8,128)} %refs_2_.3, f32[2,768,128]{2,1,0:T(8,128)} %collective-permute-done.2.left, f32[2,768,128]{2,1,0:T(8,128)} %collective-permute-done.3.right), custom_call_target="tpu_custom_call" | custom-call | tf_op jit(solution)/shard_map/local_window/pallas_call | solution.py:170
  89.0 6.7 %first.1.psi = f32[2,512,512]{2,1,0:T(8,128)S(1)} custom-call(s32[8]{0:T(128)S(1)} %concatenate.3.meta.refs_0_, f32[2,512,512]{2,1,0:T(8,128)S(1)} %copy-done.9, f32[2,128,512]{2,1,0:T(8,128)} %collective-permute-done.9.strip, f32[2,512,512]{2,1,0:T(8,128)S(1)} %copy-done.7, f32[512,512]{1,0:T(8,128)S(1)} %get-tuple-element.58.kern_re, ...), custom_call_target="tpu_custom_call" | custom-call | tf_op jit(solution)/shard_map/first/pallas_call | solution.py:320
  95.8 7.8 %second.1 = (f32[2,512,512]{2,1,0:T(8,128)S(1)}, bf16[2,512,512]{2,1,0:T(8,128)(2,1)S(1)}, f32[2,128,512]{2,1,0:T(8,128)S(1)}) custom-call(s32[8]{0:T(128)S(1)} %concatenate.3.meta.refs_0_, f32[2,512,512]{2,1,0:T(8,128)S(1)} %copy-done.8, f32[2,128,512]{2,1,0:T(8,128)} %collective-permute-done.5.strip, f32[2,512,512]{2,1,0:T(8,128)S(1)} %first.1.psi, ...), custom_call_target="tpu_custom_call" | custom-call | tf_op jit(solution)/shard_map/second/pallas_call | solution.py:320
  104.9 6.0 %third.1 = (f32[2,512,512]{2,1,0:T(8,128)S(1)}, f32[2,128,512]{2,1,0:T(8,128)S(1)}) custom-call(s32[8]{0:T(128)S(1)} %concatenate.3.meta.refs_0_, bf16[2,512,512]{2,1,0:T(8,128)(2,1)S(1)} %get-tuple-element.64.back, f32[2,512,512]{2,1,0:T(8,128)S(1)} %copy-done.7, f32[512,512]{1,0:T(8,128)S(1)} %get-tuple-element.58.kern_re, ...), custom_call_target="tpu_custom_call" | custom-call | tf_op jit(solution)/shard_map/third/pallas_call | solution.py:320
  111.4 5.5 %collective-permute-done.14.mate.refs_4_ = f32[2,128,512]{2,1,0:T(8,128)S(1)} collective-permute-done((f32[2,128,512]{2,1,0:T(8,128)S(1)}, f32[2,128,512]{2,1,0:T(8,128)S(1)}, u32[]{:S(2)}, u32[]{:S(2)}) %collective-permute-start.14) | collective-permute-done | bytes 524320 | tf_op jit(solution)/shard_map/ppermute | solution.py:479
  116.9 3.3 %collective-permute-start.15 = (f32[2,128,512]{2,1,0:T(8,128)S(1)}, f32[2,128,512]{2,1,0:T(8,128)S(1)}, u32[]{:S(2)}, u32[]{:S(2)}) collective-permute-start(f32[2,128,512]{2,1,0:T(8,128)S(1)} %collective-permute-done.14.mate.refs_4_), channel_id=1, source_target_pairs={{0,32},{32,64},{64,96},{48,16},{80,48},{112,80},{1,33},{33,65},{65... | collective-permute-start | bytes 1572872 | tf_op jit(solution)/shard_map/ppermute | solution.py:480
  120.2 7.9 %collective-permute-done.10.mate.refs_4_ = f32[2,128,512]{2,1,0:T(8,128)S(1)} collective-permute-done((f32[2,128,512]{2,1,0:T(8,128)S(1)}, f32[2,128,512]{2,1,0:T(8,128)S(1)}, u32[]{:S(2)}, u32[]{:S(2)}) %collective-permute-start.10) | collective-permute-done | bytes 524320 | tf_op jit(solution)/shard_map/ppermute | solution.py:479
  128.1 3.3 %collective-permute-start.11 = (f32[2,128,512]{2,1,0:T(8,128)S(1)}, f32[2,128,512]{2,1,0:T(8,128)S(1)}, u32[]{:S(2)}, u32[]{:S(2)}) collective-permute-start(f32[2,128,512]{2,1,0:T(8,128)S(1)} %collective-permute-done.10.mate.refs_4_), channel_id=1, source_target_pairs={{0,32},{32,64},{64,96},{48,16},{80,48},{112,80},{1,33},{33,65},{65... | collective-permute-start | bytes 1572872 | tf_op jit(solution)/shard_map/ppermute | solution.py:480
  132.3 4.5 %collective-permute-start.16 = (f32[2,768,128]{2,1,0:T(8,128)S(1)}, f32[2,768,128]{2,1,0:T(8,128)S(1)}, u32[]{:S(2)}, u32[]{:S(2)}) collective-permute-start(f32[2,768,128]{2,1,0:T(8,128)S(1)} %get-tuple-element.71), channel_id=1, source_target_pairs={{0,1},{1,2},{2,3},{3,4},{4,5},{5,6},{6,7},{7,8},{8,9},{9,10},{10,1... | collective-permute-start | bytes 2359304 | tf_op jit(solution)/shard_map/ppermute | solution.py:482
  138.7 3.4 %collective-permute-done.11.far.refs_5_ = f32[2,128,512]{2,1,0:T(8,128)S(1)} collective-permute-done((f32[2,128,512]{2,1,0:T(8,128)S(1)}, f32[2,128,512]{2,1,0:T(8,128)S(1)}, u32[]{:S(2)}, u32[]{:S(2)}) %collective-permute-start.11) | collective-permute-done | bytes 524320 | tf_op jit(solution)/shard_map/ppermute | solution.py:480
  142.9 3.8 %collective-permute-start.12 = (f32[2,768,128]{2,1,0:T(8,128)S(1)}, f32[2,768,128]{2,1,0:T(8,128)S(1)}, u32[]{:S(2)}, u32[]{:S(2)}) collective-permute-start(f32[2,768,128]{2,1,0:T(8,128)S(1)} %get-tuple-element.67), channel_id=1, source_target_pairs={{0,1},{1,2},{2,3},{3,4},{4,5},{5,6},{6,7},{7,8},{8,9},{9,10},{10,1... | collective-permute-start | bytes 2359304 | tf_op jit(solution)/shard_map/ppermute | solution.py:482
  146.7 2.3 %collective-permute-start.13 = (f32[2,768,128]{2,1,0:T(8,128)S(1)}, f32[2,768,128]{2,1,0:T(8,128)S(1)}, u32[]{:S(2)}, u32[]{:S(2)}) collective-permute-start(f32[2,768,128]{2,1,0:T(8,128)S(1)} %get-tuple-element.68), channel_id=1, source_target_pairs={{1,0},{2,1},{3,2},{4,3},{5,4},{6,5},{7,6},{8,7},{9,8},{10,9},{11,1... | collective-permute-start | bytes 2359304 | tf_op jit(solution)/shard_map/ppermute | solution.py:483
  149.0 5.1 %collective-permute-done.16.refs_6_ = f32[2,768,128]{2,1,0:T(8,128)S(1)} collective-permute-done((f32[2,768,128]{2,1,0:T(8,128)S(1)}, f32[2,768,128]{2,1,0:T(8,128)S(1)}, u32[]{:S(2)}, u32[]{:S(2)}) %collective-permute-start.16) | collective-permute-done | bytes 786464 | tf_op jit(solution)/shard_map/ppermute | solution.py:482
  154.1 11.7 %collective-permute-done.17.refs_7_ = f32[2,768,128]{2,1,0:T(8,128)S(1)} collective-permute-done((f32[2,768,128]{2,1,0:T(8,128)S(1)}, f32[2,768,128]{2,1,0:T(8,128)S(1)}, u32[]{:S(2)}, u32[]{:S(2)}) %collective-permute-start.17) | collective-permute-done | bytes 786464 | tf_op jit(solution)/shard_map/ppermute | solution.py:483
  165.8 3.1 %update.2.refs_8_ = f32[2,2,768,768]{3,2,1,0:T(8,128)} custom-call(s32[8]{0:T(128)S(1)} %concatenate.3.meta.refs_0_, f32[2]{0:T(128)S(1)} %copy-done.12, f32[2,2,768,768]{3,2,1,0:T(8,128)S(1)} %bitcast.14, f32[2,512,512]{2,1,0:T(8,128)S(1)} %get-tuple-element.69.g.refs_3_, f32[2,128,512]{2,1,0:T(8,128)S(1)} %collective-permute-done.14.mate.refs_4_, ...), custom_call_target="tpu_custom_call" | custom-call | tf_op jit(solution)/shard_map/update/pallas_call | solution.py:411
  171.0 3.3 %collective-permute-done.13.refs_7_ = f32[2,768,128]{2,1,0:T(8,128)S(1)} collective-permute-done((f32[2,768,128]{2,1,0:T(8,128)S(1)}, f32[2,768,128]{2,1,0:T(8,128)S(1)}, u32[]{:S(2)}, u32[]{:S(2)}) %collective-permute-start.13) | collective-permute-done | bytes 786464 | tf_op jit(solution)/shard_map/ppermute | solution.py:483
  174.2 3.1 %update.3 = f32[2,2,768,768]{3,2,1,0:T(8,128)} custom-call(s32[8]{0:T(128)S(1)} %concatenate.3.meta.refs_0_, f32[2]{0:T(128)S(1)} %copy-done.12, f32[2,2,768,768]{3,2,1,0:T(8,128)S(1)} %bitcast.14, f32[2,512,512]{2,1,0:T(8,128)S(1)} %get-tuple-element.65.g.refs_3_, ...), custom_call_target="tpu_custom_call", output_to_operand_aliasing={{}: (8, {})} | custom-call | tf_op jit(solution)/shard_map/update/pallas_call | solution.py:411
  (60 shorter events, 26.4 us)
Async XLA Ops:
  0.0 15.8 %copy-start.14 = (f32[512,512]{1,0:T(8,128)S(1)}, f32[512,512]{1,0:T(8,128)}, u32[]{:S(2)}) copy-start(f32[512,512]{1,0:T(8,128)} %param.9) | copy-start | bytes 3145732
  0.0 28.5 %collective-permute-start.1 = (s32[2]{0:T(128)}, s32[2]{0:T(128)S(1)}, u32[]{:S(2)}, u32[]{:S(2)}) collective-permute-start(s32[2]{0:T(128)} %bitcast.16), channel_id=1, source_target_pairs={{16,32},{48,64},{80,96},{32,16},{64,48},{96,80},{17,33},{49,65},{8... | collective-permute-start | bytes 32 | tf_op jit(solution)/shard_map/ppermute | solution.py:441
  3.6 24.8 %collective-permute-start = (s32[2]{0:T(128)}, s32[2]{0:T(128)S(1)}, u32[]{:S(2)}, u32[]{:S(2)}) collective-permute-start(s32[2]{0:T(128)} %bitcast.17), channel_id=1, source_target_pairs={{0,16},{16,0},{32,48},{48,32},{64,80},{80,64},{96,112},{112,96},{1... | collective-permute-start | bytes 32 | tf_op jit(solution)/shard_map/ppermute | solution.py:441
  7.2 12.4 %copy-start.10 = (f32[2,512,512]{2,1,0:T(8,128)S(1)}, f32[2,512,512]{2,1,0:T(8,128)}, u32[]{:S(2)}) copy-start(f32[2,512,512]{2,1,0:T(8,128)} %probe.1) | copy-start | bytes 6291460
  7.2 12.4 %copy-start.13 = (s32[1,1,1,2]{3,2,1,0:T(1,128)S(1)}, s32[1,1,1,2]{3,2,1,0:T(1,128)}, u32[]{:S(2)}) copy-start(s32[1,1,1,2]{3,2,1,0:T(1,128)} %param.11) | copy-start | bytes 28
  7.2 37.8 %collective-permute-start.6 = (f32[2,768,128]{2,1,0:T(8,128)}, f32[2,768,128]{2,1,0:T(8,128)}, u32[]{:S(2)}, u32[]{:S(2)}) collective-permute-start(f32[2,768,128]{2,1,0:T(8,128)} %get-tuple-element.48), channel_id=1, source_target_pairs={{0,1},{1,2},{2,3},{3,4},{4,5},{5,6},{6,7},{7,8},{8,9},{9,10},{10,1... | collective-permute-start | bytes 2359304 | tf_op jit(solution)/shard_map/ppermute | solution.py:438
  13.9 31.0 %collective-permute-start.7 = (f32[2,768,128]{2,1,0:T(8,128)}, f32[2,768,128]{2,1,0:T(8,128)}, u32[]{:S(2)}, u32[]{:S(2)}) collective-permute-start(f32[2,768,128]{2,1,0:T(8,128)} %get-tuple-element.49), channel_id=1, source_target_pairs={{1,0},{2,1},{3,2},{4,3},{5,4},{6,5},{7,6},{8,7},{9,8},{10,9},{11,1... | collective-permute-start | bytes 2359304 | tf_op jit(solution)/shard_map/ppermute | solution.py:439
  31.1 22.8 %collective-permute-start.2 = (f32[2,768,128]{2,1,0:T(8,128)}, f32[2,768,128]{2,1,0:T(8,128)}, u32[]{:S(2)}, u32[]{:S(2)}) collective-permute-start(f32[2,768,128]{2,1,0:T(8,128)} %get-tuple-element.46), channel_id=1, source_target_pairs={{0,1},{1,2},{2,3},{3,4},{4,5},{5,6},{6,7},{7,8},{8,9},{9,10},{10,1... | collective-permute-start | bytes 2359304 | tf_op jit(solution)/shard_map/ppermute | solution.py:438
  36.2 19.3 %collective-permute-start.3 = (f32[2,768,128]{2,1,0:T(8,128)}, f32[2,768,128]{2,1,0:T(8,128)}, u32[]{:S(2)}, u32[]{:S(2)}) collective-permute-start(f32[2,768,128]{2,1,0:T(8,128)} %get-tuple-element.47), channel_id=1, source_target_pairs={{1,0},{2,1},{3,2},{4,3},{5,4},{6,5},{7,6},{8,7},{9,8},{10,9},{11,1... | collective-permute-start | bytes 2359304 | tf_op jit(solution)/shard_map/ppermute | solution.py:439
  47.2 13.8 %collective-permute-start.8 = (f32[2,128,512]{2,1,0:T(8,128)S(1)}, f32[2,128,512]{2,1,0:T(8,128)S(1)}, u32[]{:S(2)}, u32[]{:S(2)}) collective-permute-start(f32[2,128,512]{2,1,0:T(8,128)S(1)} %far_strip.3), channel_id=1, source_target_pairs={{32,0},{64,32},{96,64},{16,48},{48,80},{80,112},{33,1},{65,33},{97... | collective-permute-start | bytes 1572872 | tf_op jit(solution)/shard_map/ppermute | solution.py:459
  57.7 16.0 %collective-permute-start.4 = (f32[2,128,512]{2,1,0:T(8,128)S(1)}, f32[2,128,512]{2,1,0:T(8,128)S(1)}, u32[]{:S(2)}, u32[]{:S(2)}) collective-permute-start(f32[2,128,512]{2,1,0:T(8,128)S(1)} %far_strip.2), channel_id=1, source_target_pairs={{32,0},{64,32},{96,64},{16,48},{48,80},{80,112},{33,1},{65,33},{97... | collective-permute-start | bytes 1572872 | tf_op jit(solution)/shard_map/ppermute | solution.py:459
  64.0 23.2 %collective-permute-start.9 = (f32[2,128,512]{2,1,0:T(8,128)}, f32[2,128,512]{2,1,0:T(8,128)}, u32[]{:S(2)}, u32[]{:S(2)}) collective-permute-start(f32[2,128,512]{2,1,0:T(8,128)} %mate_strip.3), channel_id=1, source_target_pairs={{0,16},{16,0},{32,48},{48,32},{64,80},{80,64},{96,112},{112,96},{1... | collective-permute-start | bytes 1572872 | tf_op jit(solution)/shard_map/ppermute | solution.py:460
  76.7 19.0 %collective-permute-start.5 = (f32[2,128,512]{2,1,0:T(8,128)}, f32[2,128,512]{2,1,0:T(8,128)}, u32[]{:S(2)}, u32[]{:S(2)}) collective-permute-start(f32[2,128,512]{2,1,0:T(8,128)} %mate_strip.2), channel_id=1, source_target_pairs={{0,16},{16,0},{32,48},{48,32},{64,80},{80,64},{96,112},{112,96},{1... | collective-permute-start | bytes 1572872 | tf_op jit(solution)/shard_map/ppermute | solution.py:460
  82.0 5.2 %copy-start.1 = (bf16[1024,512]{1,0:T(8,128)(2,1)S(1)}, bf16[1024,512]{1,0:T(8,128)(2,1)}, u32[]{:S(2)}) copy-start(bf16[1024,512]{1,0:T(8,128)(2,1)} %copy-done) | copy-start | bytes 3145732
  82.0 5.2 %copy-start.3 = (bf16[512,1024]{1,0:T(8,128)(2,1)S(1)}, bf16[512,1024]{1,0:T(8,128)(2,1)}, u32[]{:S(2)}) copy-start(bf16[512,1024]{1,0:T(8,128)(2,1)} %copy-done.2) | copy-start | bytes 3145732
  82.0 5.2 %copy-start.5 = (bf16[1024,512]{1,0:T(8,128)(2,1)S(1)}, bf16[1024,512]{1,0:T(8,128)(2,1)}, u32[]{:S(2)}) copy-start(bf16[1024,512]{1,0:T(8,128)(2,1)} %copy-done.4) | copy-start | bytes 3145732
  82.0 5.2 %copy-start.7 = (f32[2,512,512]{2,1,0:T(8,128)S(1)}, f32[2,512,512]{2,1,0:T(8,128)}, u32[]{:S(2)}) copy-start(f32[2,512,512]{2,1,0:T(8,128)} %copy-done.6) | copy-start | bytes 6291460
  87.2 8.5 %copy-start.8 = (f32[2,512,512]{2,1,0:T(8,128)S(1)}, f32[2,512,512]{2,1,0:T(8,128)}, u32[]{:S(2)}) copy-start(f32[2,512,512]{2,1,0:T(8,128)} %local_window.2.local) | copy-start | bytes 6291460
  87.3 1.7 copy-start.9
  89.0 6.7 %copy-start.11 = (bf16[1,1,1,512,512]{4,3,2,1,0:T(8,128)(2,1)S(1)}, bf16[1,1,1,512,512]{4,3,2,1,0:T(8,128)(2,1)}, u32[]{:S(2)}) copy-start(bf16[1,1,1,512,512]{4,3,2,1,0:T(8,128)(2,1)} %param.10) | copy-start | bytes 1572868
  95.7 70.1 %slice-start = ((s8[9437184]{0:T(1024)(128)(4,1)}), s8[4194304]{0:T(1024)(128)(4,1)S(1)}, s32[]{:S(2)}) async-start(s8[9437184]{0:T(1024)(128)(4,1)} %bitcast.13), calls=%async_computation | async-start | bytes 8388608
  95.8 70.1 %slice-start.1 = ((s8[9437184]{0:T(1024)(128)(4,1)}), s8[4194304]{0:T(1024)(128)(4,1)S(1)}, s32[]{:S(2)}) async-start(s8[9437184]{0:T(1024)(128)(4,1)} %bitcast.13), calls=%async_computation.1 | async-start | bytes 8388608
  103.5 13.3 %collective-permute-start.14 = (f32[2,128,512]{2,1,0:T(8,128)S(1)}, f32[2,128,512]{2,1,0:T(8,128)S(1)}, u32[]{:S(2)}, u32[]{:S(2)}) collective-permute-start(f32[2,128,512]{2,1,0:T(8,128)S(1)} %get-tuple-element.70), channel_id=1, source_target_pairs={{0,16},{16,0},{32,48},{48,32},{64,80},{80,64},{96,112},{112,96},{1... | collective-permute-start | bytes 1572872 | tf_op jit(solution)/shard_map/ppermute | solution.py:479
  104.9 60.9 %slice-start.2 = ((s8[9437184]{0:T(1024)(128)(4,1)}), s8[1048576]{0:T(1024)(128)(4,1)S(1)}, s32[]{:S(2)}) async-start(s8[9437184]{0:T(1024)(128)(4,1)} %bitcast.13), calls=%async_computation.2 | async-start | bytes 2097152
  110.9 17.2 %collective-permute-start.10 = (f32[2,128,512]{2,1,0:T(8,128)S(1)}, f32[2,128,512]{2,1,0:T(8,128)S(1)}, u32[]{:S(2)}, u32[]{:S(2)}) collective-permute-start(f32[2,128,512]{2,1,0:T(8,128)S(1)} %get-tuple-element.66), channel_id=1, source_target_pairs={{0,16},{16,0},{32,48},{48,32},{64,80},{80,64},{96,112},{112,96},{1... | collective-permute-start | bytes 1572872 | tf_op jit(solution)/shard_map/ppermute | solution.py:479
  116.9 14.5 %collective-permute-start.15 = (f32[2,128,512]{2,1,0:T(8,128)S(1)}, f32[2,128,512]{2,1,0:T(8,128)S(1)}, u32[]{:S(2)}, u32[]{:S(2)}) collective-permute-start(f32[2,128,512]{2,1,0:T(8,128)S(1)} %collective-permute-done.14.mate.refs_4_), channel_id=1, source_target_pairs={{0,32},{32,64},{64,96},{48,16},{80,48},{112,80},{1,33},{33,65},{65... | collective-permute-start | bytes 1572872 | tf_op jit(solution)/shard_map/ppermute | solution.py:480
  128.1 14.0 %collective-permute-start.11 = (f32[2,128,512]{2,1,0:T(8,128)S(1)}, f32[2,128,512]{2,1,0:T(8,128)S(1)}, u32[]{:S(2)}, u32[]{:S(2)}) collective-permute-start(f32[2,128,512]{2,1,0:T(8,128)S(1)} %collective-permute-done.10.mate.refs_4_), channel_id=1, source_target_pairs={{0,32},{32,64},{64,96},{48,16},{80,48},{112,80},{1,33},{33,65},{65... | collective-permute-start | bytes 1572872 | tf_op jit(solution)/shard_map/ppermute | solution.py:480
  132.3 33.6 %copy-start.12 = (f32[2]{0:T(128)S(1)}, f32[2]{0:T(128)}, u32[]{:S(2)}) copy-start(f32[2]{0:T(128)} %refs_1_.3) | copy-start | bytes 28
  132.3 21.8 %collective-permute-start.16 = (f32[2,768,128]{2,1,0:T(8,128)S(1)}, f32[2,768,128]{2,1,0:T(8,128)S(1)}, u32[]{:S(2)}, u32[]{:S(2)}) collective-permute-start(f32[2,768,128]{2,1,0:T(8,128)S(1)} %get-tuple-element.71), channel_id=1, source_target_pairs={{0,1},{1,2},{2,3},{3,4},{4,5},{5,6},{6,7},{7,8},{8,9},{9,10},{10,1... | collective-permute-start | bytes 2359304 | tf_op jit(solution)/shard_map/ppermute | solution.py:482
  136.8 29.1 %collective-permute-start.17 = (f32[2,768,128]{2,1,0:T(8,128)S(1)}, f32[2,768,128]{2,1,0:T(8,128)S(1)}, u32[]{:S(2)}, u32[]{:S(2)}) collective-permute-start(f32[2,768,128]{2,1,0:T(8,128)S(1)} %get-tuple-element.72), channel_id=1, source_target_pairs={{1,0},{2,1},{3,2},{4,3},{5,4},{6,5},{7,6},{8,7},{9,8},{10,9},{11,1... | collective-permute-start | bytes 2359304 | tf_op jit(solution)/shard_map/ppermute | solution.py:483
  142.9 28.0 %collective-permute-start.12 = (f32[2,768,128]{2,1,0:T(8,128)S(1)}, f32[2,768,128]{2,1,0:T(8,128)S(1)}, u32[]{:S(2)}, u32[]{:S(2)}) collective-permute-start(f32[2,768,128]{2,1,0:T(8,128)S(1)} %get-tuple-element.67), channel_id=1, source_target_pairs={{0,1},{1,2},{2,3},{3,4},{4,5},{5,6},{6,7},{7,8},{8,9},{9,10},{10,1... | collective-permute-start | bytes 2359304 | tf_op jit(solution)/shard_map/ppermute | solution.py:482
  146.7 27.5 %collective-permute-start.13 = (f32[2,768,128]{2,1,0:T(8,128)S(1)}, f32[2,768,128]{2,1,0:T(8,128)S(1)}, u32[]{:S(2)}, u32[]{:S(2)}) collective-permute-start(f32[2,768,128]{2,1,0:T(8,128)S(1)} %get-tuple-element.68), channel_id=1, source_target_pairs={{1,0},{2,1},{3,2},{4,3},{5,4},{6,5},{7,6},{8,7},{9,8},{10,9},{11,1... | collective-permute-start | bytes 2359304 | tf_op jit(solution)/shard_map/ppermute | solution.py:483
  (4 other events, 4.3 us)
